TPU v7x, 32 devices: a whole 2x2x4 slice. The times are simulated.
32 devices in a mesh: seq: 4 (over y, core), fsdp: 8 (over z, x).
Axes of the slice: x: 2, y: 2, z: 4, core: 2. Of those that a mesh axis runs over, the one named last changes fastest.
Arguments:
- layer_input: bfloat16 [8, 2048, 1024], P('fsdp', 'seq'), may hold values from -19 to 19
- w_qkv: bfloat16 [1024, 3072], P(('seq', 'fsdp')), may hold values from -0.1875 to 0.1875
- w_out: bfloat16 [1024, 1024], P(('seq', 'fsdp')), may hold values from -1 to 1
- w_up: bfloat16 [1024, 4096], P(('seq', 'fsdp')), may hold values from -0.1875 to 0.1875
- w_down: bfloat16 [4096, 1024], P(('seq', 'fsdp')), may hold values from -0.09375 to 0.09375
- gain_attn: bfloat16 [1024], P(('seq', 'fsdp')), may hold values from 0.099609375 to 1.8984375
- gain_mlp: bfloat16 [1024], P(('seq', 'fsdp')), may hold values from 0.099609375 to 1.8984375
- out_grad: bfloat16 [8, 2048, 1024], P('fsdp', 'seq'), may hold values from -6 to 6
- moment_qkv: float32 [1024, 3072], P(('seq', 'fsdp')), may hold values from -40 to 40
- square_qkv: float32 [1024, 3072], P(('seq', 'fsdp')), may hold values from 108.1344 to 434.176
- moment_out: float32 [1024, 1024], P(('seq', 'fsdp')), may hold values from -6 to 6
- square_out: float32 [1024, 1024], P(('seq', 'fsdp')), may hold values from 2.78528 to 11.14112
- moment_up: float32 [1024, 4096], P(('seq', 'fsdp')), may hold values from -32 to 32
- square_up: float32 [1024, 4096], P(('seq', 'fsdp')), may hold values from 52.4288 to 212.992
- moment_down: float32 [4096, 1024], P(('seq', 'fsdp')), may hold values from -48 to 48
- square_down: float32 [4096, 1024], P(('seq', 'fsdp')), may hold values from 155.648 to 622.592
- moment_gattn: float32 [1024], P(('seq', 'fsdp')), may hold values from -80 to 80
- square_gattn: float32 [1024], P(('seq', 'fsdp')), may hold values from 434.176 to 1736.704
- moment_gmlp: float32 [1024], P(('seq', 'fsdp')), may hold values from -64 to 64
- square_gmlp: float32 [1024], P(('seq', 'fsdp')), may hold values from 212.992 to 851.968
Outputs:
- layer_output: bfloat16 [8, 2048, 1024], P('fsdp', 'seq')
- input_grad: bfloat16 [8, 2048, 1024], P('fsdp', 'seq')
- grad_qkv: float32 [1024, 3072], P(('seq', 'fsdp'))
- grad_out: float32 [1024, 1024], P(('seq', 'fsdp'))
- grad_up: float32 [1024, 4096], P(('seq', 'fsdp'))
- grad_down: float32 [4096, 1024], P(('seq', 'fsdp'))
- grad_gattn: float32 [1024], P(('seq', 'fsdp'))
- grad_gmlp: float32 [1024], P(('seq', 'fsdp'))
- next_moment_qkv: float32 [1024, 3072], P(('seq', 'fsdp'))
- next_moment_out: float32 [1024, 1024], P(('seq', 'fsdp'))
- next_moment_up: float32 [1024, 4096], P(('seq', 'fsdp'))
- next_moment_down: float32 [4096, 1024], P(('seq', 'fsdp'))
- next_moment_gattn: float32 [1024], P(('seq', 'fsdp'))
- next_moment_gmlp: float32 [1024], P(('seq', 'fsdp'))
- next_square_qkv: float32 [1024, 3072], P(('seq', 'fsdp'))
- next_square_out: float32 [1024, 1024], P(('seq', 'fsdp'))
- next_square_up: float32 [1024, 4096], P(('seq', 'fsdp'))
- next_square_down: float32 [4096, 1024], P(('seq', 'fsdp'))
- next_square_gattn: float32 [1024], P(('seq', 'fsdp'))
- next_square_gmlp: float32 [1024], P(('seq', 'fsdp'))
- change_qkv: float32 [1024, 3072], P(('seq', 'fsdp'))
- change_out: float32 [1024, 1024], P(('seq', 'fsdp'))
- change_up: float32 [1024, 4096], P(('seq', 'fsdp'))
- change_down: float32 [4096, 1024], P(('seq', 'fsdp'))
- change_gattn: float32 [1024], P(('seq', 'fsdp'))
- change_gmlp: float32 [1024], P(('seq', 'fsdp'))
All inputs are finite; a program needn't handle non-finite values.
Results may differ from a plain program's by a relative error of at most 0.0089.
Values may be sent and summed in bfloat16 or wider, within the bound.
No kernel may reach another device: no remote copies, remote signals or barrier semaphores. Data moves between devices by JAX's collectives and lax.ppermute only.
A program may use at most 192 MiB of HBM per device.

v0:
```python
import functools
import jax
import jax.numpy as jnp
from jax import lax
from jax.experimental import pallas as pl
from jax.experimental.pallas import tpu as pltpu
from jax.sharding import PartitionSpec as P


F32 = jnp.float32
BF16 = jnp.bfloat16
EPS_NORM = 1e-05
HD = 64
ROT = 16
PAIR = 2 * HD
STEP = 10
BETA_ONE = 0.9
BETA_TWO = 0.95
RATE = 0.02
DECAY = 0.1
ADAM_EPS = 1e-08


def contract_last(left, right):
    return lax.dot_general(left, right, (((1,), (1,)), ((), ())), preferred_element_type=F32)


def contract_first(left, right):
    return lax.dot_general(left, right, (((0,), (0,)), ((), ())), preferred_element_type=F32)


def plain_dot(left, right):
    return lax.dot_general(left, right, (((1,), (0,)), ((), ())), preferred_element_type=F32)


def turn(pair_values, cosine, sine):
    lane = lax.broadcasted_iota(jnp.int32, (1, PAIR), 1)
    ahead = pltpu.roll(pair_values, PAIR - ROT // 2, 1)
    behind = pltpu.roll(pair_values, ROT // 2, 1)
    return pair_values * cosine + jnp.where(lane % HD < ROT // 2, -ahead, behind) * sine


def place(i, me, count):
    return ((i // count) ^ me[0]) * count + i % count


def piece_specs(pieces, block):
    count = pieces[0].shape[0] // block

    def spec(k):
        return pl.BlockSpec(
            (block, pieces[0].shape[1]), lambda i, me: (jnp.clip(i - k * count, 0, count - 1), 0)
        )

    return [spec(k) for k in range(len(pieces))]


def take_piece(refs, held, count):
    step = pl.program_id(0)
    for k, ref in enumerate(refs):

        @pl.when(step // count == k)
        def _():
            held[...] = ref[...]

    return held[...]


def normalize(rows, gain):
    centred = rows - jnp.mean(rows, axis=-1, keepdims=True)
    spread = jnp.mean(centred * centred, axis=-1, keepdims=True)
    return (centred * lax.rsqrt(spread + EPS_NORM) * gain).astype(BF16)


def project_kernel(count, me, x0, x1, x2, x3, ga_ref, w_ref, cos_ref, sin_ref, na_ref, qkv_ref, held):
    rows = take_piece((x0, x1, x2, x3), held, count).astype(F32)
    normed = normalize(rows, ga_ref[...])
    na_ref[...] = normed
    projected = plain_dot(normed, w_ref[...])
    width = w_ref.shape[1] // 3
    cosine = cos_ref[...]
    sine = sin_ref[...]
    for start in range(0, 3 * width, PAIR):
        columns = projected[:, start : start + PAIR]
        kind = start // PAIR % 3
        if kind < 2:
            columns = turn(columns, cosine, sine)
        columns = columns.astype(BF16)
        if kind == 0:
            columns = columns * jnp.asarray(HD**-0.5, BF16)
        qkv_ref[:, start : start + PAIR] = columns


def project(me, pieces, gain_attn, weight, tables, block=256):
    tokens, dim = pieces[0].shape
    count = tokens // block
    length = 4 * tokens
    width = weight.shape[1]
    whole = lambda i, me: (0, 0)
    part = lambda i, me: (place(i, me, count), 0)
    return pl.pallas_call(
        functools.partial(project_kernel, count),
        name="project",
        grid_spec=pltpu.PrefetchScalarGridSpec(
            num_scalar_prefetch=1,
            grid=(length // block,),
            in_specs=piece_specs(pieces, block)
            + [
                pl.BlockSpec((1, dim), whole),
                pl.BlockSpec((dim, width), whole),
                pl.BlockSpec((block, PAIR), part),
                pl.BlockSpec((block, PAIR), part),
            ],
            out_specs=[
                pl.BlockSpec((block, dim), part),
                pl.BlockSpec((block, width), part),
            ],
            scratch_shapes=[pltpu.VMEM((block, dim), BF16)],
        ),
        out_shape=[
            jax.ShapeDtypeStruct((length, dim), BF16),
            jax.ShapeDtypeStruct((length, width), BF16),
        ],
        cost_estimate=pl.CostEstimate(
            flops=2 * length * dim * width, bytes_accessed=6 * length * dim + 2 * length * width, transcendentals=0
        ),
    )(me, *pieces, gain_attn, weight, *tables)


def forward_kernel(block, q_ref, k_ref, v_ref, o_ref, lse_ref, v_first, v_second):
    at = pl.program_id(1)
    lane = lax.broadcasted_iota(jnp.int32, (1, PAIR), 1)
    first = lane < HD

    @pl.when(at == 0)
    def _():
        values = v_ref[...]
        one = jnp.ones_like(values)
        v_first[...] = jnp.where(first, values, one)
        v_second[...] = jnp.where(first, one, values)

    queries = q_ref[...]
    nil = jnp.zeros_like(queries)
    q_first = jnp.where(first, queries, nil)
    q_second = jnp.where(first, nil, queries)

    def one_head(q_part, v_part, start, masked, top, total):
        keys = k_ref[pl.ds(start, block), :]
        scores = contract_last(q_part, keys)
        if masked:
            row = lax.broadcasted_iota(jnp.int32, scores.shape, 0)
            col = lax.broadcasted_iota(jnp.int32, scores.shape, 1)
            scores = jnp.where(col <= row, scores, -1e30)
        new_top = jnp.maximum(top, jnp.max(scores, axis=-1, keepdims=True))
        weights = jnp.exp(scores - new_top).astype(BF16)
        total = total * jnp.exp(top - new_top) + plain_dot(weights, v_part[pl.ds(start, block), :])
        return new_top, total

    def both(j, state, masked):
        start = pl.multiple_of(j * block, block)
        top_a, sum_a, top_b, sum_b = state
        top_a, sum_a = one_head(q_first, v_first, start, masked, top_a, sum_a)
        top_b, sum_b = one_head(q_second, v_second, start, masked, top_b, sum_b)
        return top_a, sum_a, top_b, sum_b

    low = jnp.full((block, 1), -1e30, F32)
    zero = jnp.zeros((block, PAIR), F32)
    state = both(at, (low, zero, low, zero), True)
    state = lax.fori_loop(0, at, lambda j, s: both(j, s, False), state)
    top_a, sum_a, top_b, sum_b = state
    mixed = jnp.where(first, sum_a, sum_b)
    total = jnp.where(first, pltpu.roll(sum_a, HD, 1), pltpu.roll(sum_b, HD, 1))
    o_ref[...] = (mixed / total).astype(BF16)
    lse_ref[...] = jnp.where(first, top_a, top_b) + jnp.log(total)


def attend(qkv, block=512):
    length, width3 = qkv.shape
    width = width3 // 3
    pairs = width // PAIR
    steps = length // block
    return pl.pallas_call(
        functools.partial(forward_kernel, block),
        name="attend",
        grid=(pairs, steps),
        in_specs=[
            pl.BlockSpec((block, PAIR), lambda h, i: (i, 3 * h)),
            pl.BlockSpec((length, PAIR), lambda h, i: (0, 3 * h + 1)),
            pl.BlockSpec((length, PAIR), lambda h, i: (0, 3 * h + 2)),
        ],
        out_specs=[
            pl.BlockSpec((block, PAIR), lambda h, i: (i, h)),
            pl.BlockSpec((block, PAIR), lambda h, i: (i, h)),
        ],
        out_shape=[
            jax.ShapeDtypeStruct((length, width), BF16),
            jax.ShapeDtypeStruct((length, width), F32),
        ],
        scratch_shapes=[pltpu.VMEM((length, PAIR), BF16), pltpu.VMEM((length, PAIR), BF16)],
        cost_estimate=pl.CostEstimate(
            flops=8 * length * length * width, bytes_accessed=12 * length * width, transcendentals=length * length * width // HD
        ),
    )(qkv, qkv, qkv)


def backward_kernel(
    block, q_ref, k_ref, v_ref, o_ref, do_ref, lse_ref, cos_ref, sin_ref,
    grad_ref, q_a, q_b, k_a, k_b, do_a, do_b, top_row, dot_row, dq_sum,
):
    length = q_ref.shape[0]
    steps = length // block
    lane = lax.broadcasted_iota(jnp.int32, (1, PAIR), 1)
    first = lane < HD
    ones = jnp.ones((8, PAIR), BF16)
    for i in range(steps):
        at = pl.ds(i * block, block)
        nil = jnp.zeros((block, PAIR), BF16)
        for source, left, right in ((q_ref, q_a, q_b), (k_ref, k_a, k_b), (do_ref, do_a, do_b)):
            values = source[at, :]
            left[at, :] = jnp.where(first, values, nil)
            right[at, :] = jnp.where(first, nil, values)
        product = do_ref[at, :].astype(F32) * o_ref[at, :].astype(F32)
        high_part = product.astype(BF16)
        low_part = (product - high_part.astype(F32)).astype(BF16)
        for slot, keep in ((0, first), (1, jnp.logical_not(first))):
            dot_row[8 * slot : 8 * slot + 8, at] = contract_last(
                ones, jnp.where(keep, high_part, nil)
            ) + contract_last(ones, jnp.where(keep, low_part, nil))
        turned = jnp.transpose(lse_ref[at, :])
        top_row[0:8, at] = turned[0:8, :]
        top_row[8:16, at] = turned[HD : HD + 8, :]
    dq_sum[...] = jnp.zeros_like(dq_sum)

    def one_block(i, j, key_sum, value_sum, masked):
        q_at = pl.ds(pl.multiple_of(i * block, block), block)
        k_at = pl.ds(pl.multiple_of(j * block, block), block)
        keys = k_ref[k_at, :]
        values = v_ref[k_at, :]
        for slot, q_s, k_s, do_s in ((0, q_a, k_a, do_a), (1, q_b, k_b, do_b)):
            q_part = q_s[q_at, :]
            do_part = do_s[q_at, :]
            scores = contract_last(keys, q_part)
            if masked:
                key_at = lax.broadcasted_iota(jnp.int32, scores.shape, 0)
                query_at = lax.broadcasted_iota(jnp.int32, scores.shape, 1)
                scores = jnp.where(key_at <= query_at, scores, -1e30)
            soft = jnp.exp(scores - top_row[8 * slot : 8 * slot + 1, q_at])
            value_sum = value_sum + plain_dot(soft.astype(BF16), do_part)
            grad = contract_last(values, do_part)
            grad_scores = (soft * (grad - dot_row[8 * slot : 8 * slot + 1, q_at])).astype(BF16)
            key_sum = key_sum + plain_dot(grad_scores, q_part)
            dq_sum[q_at, :] += contract_first(grad_scores, k_s[k_at, :])
        return key_sum, value_sum

    def key_block(j, carry):
        zero = jnp.zeros((block, PAIR), F32)
        state = one_block(j, j, zero, zero, True)
        state = lax.fori_loop(j + 1, steps, lambda i, s: one_block(i, j, s[0], s[1], False), state)
        k_at = pl.ds(pl.multiple_of(j * block, block), block)
        grad_ref[k_at, PAIR : 2 * PAIR] = turn(state[0], cos_ref[k_at, :], -sin_ref[k_at, :]).astype(BF16)
        grad_ref[k_at, 2 * PAIR :] = state[1].astype(BF16)
        return carry

    lax.fori_loop(0, steps, key_block, 0)
    for i in range(steps):
        at = pl.ds(i * block, block)
        turned = turn(dq_sum[at, :] * HD**-0.5, cos_ref[at, :], -sin_ref[at, :])
        grad_ref[at, :PAIR] = turned.astype(BF16)


def attend_back(qkv, context, grad_context, lse, tables, pair, block=512):
    length = qkv.shape[0]
    col = lambda at: pl.BlockSpec((length, PAIR), lambda h: (0, at))
    whole = pl.BlockSpec((length, PAIR), lambda h: (0, 0))
    return pl.pallas_call(
        functools.partial(backward_kernel, block),
        name="attend_back",
        grid=(1,),
        in_specs=[col(3 * pair), col(3 * pair + 1), col(3 * pair + 2), col(pair), col(pair), col(pair), whole, whole],
        out_specs=pl.BlockSpec((length, 3 * PAIR), lambda h: (0, 0)),
        out_shape=jax.ShapeDtypeStruct((length, 3 * PAIR), BF16),
        scratch_shapes=[pltpu.VMEM((length, PAIR), BF16)] * 6
        + [pltpu.VMEM((16, length), F32)] * 2
        + [pltpu.VMEM((length, PAIR), F32)],
        cost_estimate=pl.CostEstimate(
            flops=20 * length * length * PAIR, bytes_accessed=20 * length * PAIR, transcendentals=2 * length * length
        ),
    )(qkv, qkv, qkv, context, grad_context, lse, *tables)


def mlp_kernel(
    count, me, x0, x1, x2, x3, g0, g1, g2, g3, gain_ref, down_ref, up_ref,
    n_ref, act_ref, gh_ref, g_ref, part_ref, below_ref, x_held, g_held,
):
    gain = gain_ref[...]
    normed = normalize(take_piece((x0, x1, x2, x3), x_held, count).astype(F32), gain)
    n_ref[...] = normed
    upstream = take_piece((g0, g1, g2, g3), g_held, count)
    g_ref[...] = upstream
    down = down_ref[...]
    up = up_ref[...]
    hidden = plain_dot(normed, up)
    back = contract_last(upstream, down)
    below = 0.5 + 0.5 * lax.erf(hidden * (0.5**0.5))
    activated = (hidden * below).astype(BF16)
    slope = below + hidden * jnp.exp(-0.5 * hidden * hidden) * 0.3989422804014327
    grad_hidden = (back * slope).astype(BF16)
    act_ref[...] = activated
    gh_ref[...] = grad_hidden
    part_ref[...] = plain_dot(activated, down).astype(BF16)
    below_ref[...] = (contract_last(grad_hidden, up) * gain).astype(BF16)


def mlp(me, pieces, grad_pieces, gain_mlp, w_down, w_up, block=256):
    tokens, dim = pieces[0].shape
    length = 4 * tokens
    hid = w_up.shape[1]
    count = tokens // block
    whole = lambda i, me: (0, 0)
    part = lambda i, me: (place(i, me, count), 0)
    tile = lambda columns: pl.BlockSpec((block, columns), part)
    shape = lambda columns: jax.ShapeDtypeStruct((length, columns), BF16)
    return pl.pallas_call(
        functools.partial(mlp_kernel, count),
        name="mlp",
        grid_spec=pltpu.PrefetchScalarGridSpec(
            num_scalar_prefetch=1,
            grid=(length // block,),
            in_specs=piece_specs(pieces, block)
            + piece_specs(grad_pieces, block)
            + [
                pl.BlockSpec((1, dim), whole),
                pl.BlockSpec((hid, dim), whole),
                pl.BlockSpec((dim, hid), whole),
            ],
            out_specs=[tile(dim), tile(hid), tile(hid), tile(dim), tile(dim), tile(dim)],
            scratch_shapes=[
                pltpu.VMEM((block, dim), BF16),
                pltpu.VMEM((block, dim), BF16),
            ],
        ),
        out_shape=[shape(dim), shape(hid), shape(hid), shape(dim), shape(dim), shape(dim)],
        cost_estimate=pl.CostEstimate(
            flops=8 * length * dim * hid, bytes_accessed=16 * length * dim + 4 * dim * hid, transcendentals=2 * length * hid
        ),
    )(me, *pieces, *grad_pieces, gain_mlp, w_down, w_up)


def below_kernel(first_ref, second_ref, w_ref, gain_ref, term_ref, o_ref):
    half = first_ref.shape[1]
    grad = contract_last(first_ref[...], w_ref[:, :half]) + contract_last(second_ref[...], w_ref[:, half:])
    o_ref[...] = (grad * gain_ref[...] + term_ref[...].astype(F32)).astype(BF16)


def below(first, second, weight, gain, term, block=512):
    length, half = first.shape
    dim = weight.shape[0]
    part = lambda i: (i, 0)
    whole = lambda i: (0, 0)
    return pl.pallas_call(
        below_kernel,
        name="below",
        grid=(length // block,),
        in_specs=[
            pl.BlockSpec((block, half), part),
            pl.BlockSpec((block, half), part),
            pl.BlockSpec((dim, 2 * half), whole),
            pl.BlockSpec((1, dim), whole),
            pl.BlockSpec((block, dim), part),
        ],
        out_specs=pl.BlockSpec((block, dim), part),
        out_shape=jax.ShapeDtypeStruct((length, dim), BF16),
        cost_estimate=pl.CostEstimate(
            flops=4 * length * dim * half, bytes_accessed=4 * length * dim + 4 * length * half, transcendentals=0
        ),
    )(first, second, weight, gain, term)


def swap(values, axis, bit):
    ways = lax.axis_size(axis)
    return lax.ppermute(values, axis, [(i, i ^ bit) for i in range(ways)])


def bits_of(ways):
    return [1 << k for k in range(ways.bit_length() - 1)]


def bit_set(axis, bit):
    return (lax.axis_index(axis) & bit) != 0


def pick(values, at, axis):
    return lax.dynamic_index_in_dim(values, at, axis, keepdims=False)


def gather_far_first(shard, axis, at):
    held = shard
    for bit in reversed(bits_of(lax.axis_size(axis))):
        other = swap(held, axis, bit)
        upper = bit_set(axis, bit)
        held = jnp.stack([jnp.where(upper, other, held), jnp.where(upper, held, other)], axis=at)
        at += 1
    return held


def reduce_near_first(values, axis, at):
    bits = bits_of(lax.axis_size(axis))
    held = values.reshape(values.shape[:at] + (2,) * len(bits) + values.shape[at + 1 :])
    for bit in bits:
        mine = (lax.axis_index(axis) & bit) // bit
        spot = at + len(bits) - bits.index(bit) - 1
        arrived = swap(pick(held, 1 - mine, spot), axis, bit)
        held = (pick(held, mine, spot).astype(F32) + arrived.astype(F32)).astype(BF16)
    return held


def exchange(values, axis):
    ways = lax.axis_size(axis)
    me = lax.axis_index(axis)
    pieces = [pick(values, me, 0)]
    for k in range(1, ways):
        pieces.append(swap(pick(values, me ^ k, 0), axis, k))
    count = len(bits_of(ways))
    held = jnp.stack(pieces).reshape((2,) * count + pieces[0].shape)
    for spot, bit in enumerate(reversed(bits_of(ways))):
        held = jnp.where(bit_set(axis, bit), jnp.flip(held, spot), held)
    return held.reshape((ways,) + pieces[0].shape)


def gather_sequence(rows):
    near = swap(rows, "seq", 1)
    far = swap(rows, "seq", 2)
    return rows, near, far, swap(far, "seq", 1)


def sum_sequence(partial):
    me = lax.axis_index("seq")
    tokens = partial.shape[0] // 4
    held = partial.reshape(2, 2, tokens, partial.shape[1])
    mine = me & 1
    arrived = swap(pick(held, 1 - mine, 1), "seq", 1)
    held = (pick(held, mine, 1).astype(F32) + arrived.astype(F32)).astype(BF16)
    mine = me >> 1
    arrived = swap(pick(held, 1 - mine, 0), "seq", 2)
    return pick(held, mine, 0).astype(F32) + arrived.astype(F32)


def rotary_tables(length):
    lane = jnp.arange(PAIR, dtype=jnp.int32) % HD
    step = (lane % (ROT // 2)).astype(F32)
    frequency = jnp.where(lane < ROT, 10000.0 ** (-(step * 2.0) / ROT), 0.0)
    angles = jnp.arange(length, dtype=jnp.int32).astype(F32)[:, None] * frequency[None, :]
    return jnp.cos(angles), jnp.sin(angles)


def adam_step(weight, gradient, moment, square, decay_rate):
    moment_next = BETA_ONE * moment + (1.0 - BETA_ONE) * gradient
    square_next = BETA_TWO * square + (1.0 - BETA_TWO) * gradient * gradient
    moment_hat = moment_next / (1.0 - BETA_ONE**STEP)
    square_hat = square_next / (1.0 - BETA_TWO**STEP)
    change = -RATE * (
        moment_hat / (jnp.sqrt(square_hat) + ADAM_EPS) + decay_rate * weight.astype(F32)
    )
    return (moment_next, square_next, change)


def one_step(
    layer_input, w_qkv, w_out, w_up, w_down, gain_attn, gain_mlp, out_grad,
    moment_qkv, square_qkv, moment_out, square_out, moment_up, square_up, moment_down, square_down,
    moment_gattn, square_gattn, moment_gmlp, square_gmlp,
):
    ways = lax.axis_size("seq")
    fold = lax.axis_size("fsdp")
    rows = w_qkv.shape[0]
    dim = rows * ways * fold
    inner = w_qkv.shape[1] // 3
    group = inner // ways
    hid = w_up.shape[1] // ways
    tokens = layer_input.shape[1]
    length = tokens * ways

    me = lax.axis_index("seq").astype(jnp.int32).reshape(1)
    gains = gather_far_first(
        gather_far_first(jnp.stack([gain_attn, gain_mlp]), "seq", 1), "fsdp", 3
    ).reshape(2, dim).astype(F32)
    down_rows = w_down.shape[0]
    split_up = w_up.reshape(rows, ways, hid).transpose(1, 0, 2)
    full_down = lax.all_gather(w_down, "fsdp", tiled=True)
    local_up = exchange(split_up, "seq")
    full_up = gather_far_first(local_up, "fsdp", 1).reshape(dim, hid)
    local_rows = layer_input[0]
    row_pieces = gather_sequence(local_rows)
    grad_pieces = gather_sequence(out_grad[0])
    count = group // PAIR
    split_qkv = (
        w_qkv.reshape(rows, 3, ways, count, PAIR).transpose(2, 0, 3, 1, 4).reshape(ways, rows, 3 * group)
    )
    local_qkv = exchange(split_qkv, "seq")
    flat_out = w_out.reshape(rows, ways, dim // ways).transpose(1, 0, 2)
    both = lax.all_gather(jnp.concatenate([local_qkv, flat_out], axis=2), "fsdp")
    full_qkv = both[..., : 3 * group].transpose(1, 0, 2, 3).reshape(dim, 3 * group)
    full_out = both[..., 3 * group :].transpose(0, 2, 1, 3).reshape(fold * rows, dim)
    tables = rotary_tables(length)
    gains, tables = lax.optimization_barrier((gains, tables))

    normed_mlp, activated, grad_hidden, upstream, partial, mlp_term = mlp(
        me, row_pieces, grad_pieces, gains[1:2], full_down, full_up
    )
    grad_wdown = contract_first(activated, upstream).astype(BF16)
    grad_wup = contract_first(normed_mlp, grad_hidden).astype(BF16)
    sendable = jnp.concatenate(
        [
            grad_wdown.reshape(fold, down_rows, dim),
            grad_wup.reshape(ways, fold, rows, hid).transpose(1, 0, 2, 3).reshape(fold, ways * rows, hid),
        ],
        axis=1,
    )
    sendable, full_qkv = lax.optimization_barrier((sendable, full_qkv))
    owned_sum = lax.psum_scatter(sendable, "fsdp", scatter_dimension=0)

    normed_attn, qkv = project(me, row_pieces, gains[0:1], full_qkv, tables)
    context, lse = attend(qkv)
    grad_context = contract_last(upstream, full_out).astype(BF16)
    partial = (plain_dot(context, full_out) + partial.astype(F32)).astype(BF16)
    grad_wout = contract_first(context, upstream).astype(BF16)
    grad_context, partial, grad_wout = lax.optimization_barrier((grad_context, partial, grad_wout))
    branch = sum_sequence(partial)
    layer_output = (local_rows.astype(F32) + branch).astype(BF16)[None]
    sum_out = reduce_near_first(grad_wout.reshape(fold, rows, dim), "fsdp", 0).astype(F32)

    near_pairs = []
    grad_pairs = []
    for pair in range(count):
        grad_pair = attend_back(qkv, context, grad_context, lse, tables, pair)
        if pair + 1 == count:
            grad_pair, owned_sum = lax.optimization_barrier((grad_pair, owned_sum))
        grad_weight = contract_first(normed_attn, grad_pair).astype(BF16)
        if pair + 1 < count:
            grad_weight, grad_context = lax.optimization_barrier((grad_weight, grad_context))
        near = reduce_near_first(grad_weight.reshape(ways, fold, rows, 3 * PAIR), "fsdp", 1)
        near_pairs.append(near)
        grad_pairs.append(grad_pair)
    upper = below(grad_pairs[0], grad_pairs[1], full_qkv, gains[0:1], mlp_term)
    sum_down = owned_sum[:down_rows].astype(F32)
    back_up = exchange(owned_sum[down_rows:].reshape(ways, rows, hid), "seq")
    sum_up = back_up.transpose(1, 0, 2).reshape(rows, ways * hid).astype(F32)
    near_qkv = jnp.concatenate(near_pairs, axis=2)
    back_qkv = exchange(near_qkv, "seq")
    sum_qkv = (
        back_qkv.reshape(ways, rows, count, 3, PAIR).transpose(1, 3, 0, 2, 4).reshape(rows, 3 * inner).astype(F32)
    )

    upper = sum_sequence(upper)
    local = local_rows.astype(F32)
    centred = local - jnp.mean(local, axis=-1, keepdims=True)
    inverse = lax.rsqrt(jnp.mean(centred * centred, axis=-1, keepdims=True) + EPS_NORM)
    xhat = centred * inverse
    term = inverse * (
        upper
        - jnp.mean(upper, axis=-1, keepdims=True)
        - xhat * jnp.mean(upper * xhat, axis=-1, keepdims=True)
    )
    input_grad = (out_grad[0].astype(F32) + term).astype(BF16)[None]

    sum_gattn = jnp.sum(w_qkv.astype(F32) * sum_qkv, axis=1) / gain_attn.astype(F32)
    sum_gmlp = jnp.sum(w_up.astype(F32) * sum_up, axis=1) / gain_mlp.astype(F32)
    summed = (sum_qkv, sum_out, sum_up, sum_down, sum_gattn, sum_gmlp)
    owned = (w_qkv, w_out, w_up, w_down, gain_attn, gain_mlp)
    moments = (moment_qkv, moment_out, moment_up, moment_down, moment_gattn, moment_gmlp)
    squares = (square_qkv, square_out, square_up, square_down, square_gattn, square_gmlp)
    decays = (DECAY, DECAY, DECAY, DECAY, 0.0, 0.0)
    results = [
        adam_step(owned[slot], summed[slot], moments[slot], squares[slot], decays[slot])
        for slot in range(6)
    ]
    return (
        (layer_output, input_grad)
        + summed
        + tuple(result[0] for result in results)
        + tuple(result[1] for result in results)
        + tuple(result[2] for result in results)
    )


def solution(mesh):
    acts = P("fsdp", "seq", None)
    mat = P(("seq", "fsdp"), None)
    vec = P(("seq", "fsdp"))
    six = (mat, mat, mat, mat, vec, vec)
    return jax.shard_map(
        one_step,
        mesh=mesh,
        in_specs=(acts,) + six + (acts,) + (mat,) * 8 + (vec,) * 4,
        out_specs=(acts, acts) + six * 4,
        check_vma=False,
    )
```

profile of v0, /device:TPU:0, one launch (start us, length us, event | category | flops | bytes accessed | tf_op | source)
XLA Modules:
  0.0 394.6 jit_solution(11034965298739118807)
XLA Ops:
  16.5 5.5 %multiply_sine_fusion = (f32[2048,128]{1,0:T(8,128)}, f32[2048,128]{1,0:T(8,128)}) fusion(f32[128]{0:T(128)S(1)} %compare_select_fusion.2, f32[2048]{0:T(1024)S(1)} %iota_convert_fusion), kind=kLoop, calls=%fused_computation.30 | loop fusion | flops 262144 | bytes 2105856 | tf_op jit(solution)/shard_map/sin | solution.py:453
  22.0 12.6 %collective-permute-done.6 = bf16[2,32]{1,0:T(2,128)(2,1)S(1)} collective-permute-done((bf16[2,32]{1,0:T(2,128)(2,1)S(1)}, bf16[2,32]{1,0:T(2,128)(2,1)S(1)}, u32[]{:S(2)}, u32[]{:S(2)}) %collective-permute-start.6) | collective-permute-done | bytes 160 | tf_op jit(solution)/shard_map/ppermute | solution.py:381
  36.1 21.4 %collective-permute-done.13 = bf16[32,1024]{1,0:T(8,128)(2,1)S(1)} collective-permute-done((bf16[32,1024]{1,0:T(8,128)(2,1)S(1)}, bf16[32,1024]{1,0:T(8,128)(2,1)S(1)}, u32[]{:S(2)}, u32[]{:S(2)}) %collective-permute-start.13) | collective-permute-done | bytes 65568 | tf_op jit(solution)/shard_map/ppermute | solution.py:381
  63.1 10.8 %collective-permute-done.14 = bf16[4,32,1024]{2,1,0:T(8,128)(2,1)S(1)} collective-permute-done((bf16[4,32,1024]{2,1,0:T(8,128)(2,1)S(1)}, bf16[4,32,1024]{2,1,0:T(8,128)(2,1)S(1)}, u32[]{:S(2)}, u32[]{:S(2)}) %collective-permute-start.14) | collective-permute-done | bytes 262176 | tf_op jit(solution)/shard_map/ppermute | solution.py:381
  76.3 10.9 %collective-permute-done.9 = bf16[2,2,2,2,32]{4,1,0,2,3:T(2,128)(2,1)S(1)} collective-permute-done((bf16[2,2,2,2,32]{4,1,0,2,3:T(2,128)(2,1)S(1)}, bf16[2,2,2,2,32]{4,1,0,2,3:T(2,128)(2,1)S(1)}, u32[]{:S(2)}, u32[]{:S(2)}) %collective-permute-start.9) | collective-permute-done | bytes 1056 | tf_op jit(solution)/shard_map/ppermute | solution.py:381
  96.9 21.3 %collective-permute-done.16 = bf16[4,2,2,32,1024]{4,3,2,1,0:T(8,128)(2,1)S(1)} collective-permute-done((bf16[4,2,2,32,1024]{4,3,2,1,0:T(8,128)(2,1)}, bf16[4,2,2,32,1024]{4,3,2,1,0:T(8,128)(2,1)S(1)}, u32[]{:S(2)}, u32[]{:S(2)}) %collective-permute-start.16) | collective-permute-done | bytes 1048608 | tf_op jit(solution)/shard_map/ppermute | solution.py:381
  119.9 28.3 %mlp.1 = (bf16[2048,1024]{1,0:T(8,128)(2,1)}, bf16[2048,1024]{1,0:T(8,128)(2,1)}, bf16[2048,1024]{1,0:T(8,128)(2,1)}, bf16[2048,1024]{1,0:T(8,128)(2,1)}, bf16[2...) custom-call(s32[1]{0:T(128)} %bitcast.1.me, bf16[512,1024]{1,0:T(8,128)(2,1)} %bitcast.235, ...), custom_call_target="tpu_custom_call" | custom-call | flops 17179869184 | bytes 37748736 | tf_op jit(solution)/shard_map/mlp/pallas_call | solution.py:323
  148.3 8.2 %convolution_convert_fusion.1 = bf16[1024,1024]{1,0:T(8,128)(2,1)S(1)} fusion(bf16[2048,1024]{1,0:T(8,128)(2,1)} %get-tuple-element.51, bf16[2048,1024]{1,0:T(8,128)(2,1)} %get-tuple-element.52), kind=kOutput, calls=%fused_computation.26 | convolution fusion | flops 4296015872 | bytes 10485760 | tf_op jit(solution)/shard_map/dot_general | solution.py:29
  158.7 4.8 %convolution_convert_fusion.2 = bf16[1024,1024]{1,0:T(8,128)(2,1)S(1)} fusion(bf16[2048,1024]{1,0:T(8,128)(2,1)S(1)} %copy-done.35, bf16[2048,1024]{1,0:T(8,128)(2,1)S(1)} %copy-done.34), kind=kOutput, calls=%fused_computation.27 | convolution fusion | flops 4296015872 | bytes 10485760 | tf_op jit(solution)/shard_map/dot_general | solution.py:29
  172.0 12.3 %project.1 = (bf16[2048,1024]{1,0:T(8,128)(2,1)}, bf16[2048,768]{1,0:T(8,128)(2,1)}) custom-call(s32[1]{0:T(128)} %bitcast.1.me, bf16[512,1024]{1,0:T(8,128)(2,1)} %bitcast.236, bf16[512,1024]{1,0:T(8,128)(2,1)} %collective-permute-done.x1, bf16[512,1024]{1,0:T(8,128)(2,1)} %collective-permute-done.1.x2, bf16[512,1024]{1,0:T(8,128)(2,1)} %collective-permute-done.2.x3, ...), custom_call_target="tpu_custom_call" | custom-call | flops 3221225472 | bytes 15728640 | tf_op jit(solution)/shard_map/project/pallas_call | solution.py:101
  184.4 4.5 %convolution_convert_fusion.do_ref = bf16[2048,256]{1,0:T(8,128)(2,1)} fusion(bf16[2048,1024]{1,0:T(8,128)(2,1)} %get-tuple-element.49, bf16[256,1024]{1,0:T(8,128)(2,1)S(1)} %bitcast.241), kind=kOutput, calls=%fused_computation.9 | convolution fusion | flops 1074266112 | bytes 5767168 | tf_op jit(solution)/shard_map/dot_general | solution.py:25
  188.9 26.4 %attend.1 = (bf16[2048,256]{1,0:T(8,128)(2,1)}, f32[2048,256]{1,0:T(8,128)}) custom-call(bf16[2048,768]{1,0:T(8,128)(2,1)} %get-tuple-element.56.q_ref.k_ref.v_ref, bf16[2048,768]{1,0:T(8,128)(2,1)} %get-tuple-element.56.q_ref.k_ref.v_ref, bf16[2048,768]{1,0:T(8,128)(2,1)} %get-tuple-element.56.q_ref.k_ref.v_ref), custom_call_target="tpu_custom_call" | custom-call | flops 8589934592 | bytes 6291456 | tf_op jit(solution)/shard_map/attend/pallas_call | solution.py:182
  215.3 4.7 %convolution_convert_fusion.5 = bf16[256,1024]{1,0:T(8,128)(2,1)} fusion(bf16[2048,256]{1,0:T(8,128)(2,1)} %get-tuple-element.57.o_ref, bf16[2048,1024]{1,0:T(8,128)(2,1)} %get-tuple-element.49), kind=kOutput, calls=%fused_computation.34 | convolution fusion | flops 1074003968 | bytes 5767168 | tf_op jit(solution)/shard_map/dot_general | solution.py:29
  223.3 23.5 %attend_back.2.first_ref = bf16[2048,384]{1,0:T(8,128)(2,1)} custom-call(bf16[2048,768]{1,0:T(8,128)(2,1)} %get-tuple-element.56.q_ref.k_ref.v_ref, bf16[2048,768]{1,0:T(8,128)(2,1)} %get-tuple-element.56.q_ref.k_ref.v_ref, bf16[2048,768]{1,0:T(8,128)(2,1)} %get-tuple-element.56.q_ref.k_ref.v_ref, bf16[2048,256]{1,0:T(8,128)(2,1)} %get-tuple-element.57.o_ref, ...), custom_call_target="tpu_custom_call" | custom-call | flops 10737418240 | bytes 5242880 | tf_op jit(solution)/shard_map/attend_back/pallas_call | solution.py:275
  246.7 5.2 %convolution_convert_fusion.4 = bf16[1024,384]{1,0:T(8,128)(2,1)S(1)} fusion(bf16[2048,1024]{1,0:T(8,128)(2,1)} %get-tuple-element.62, bf16[2048,384]{1,0:T(8,128)(2,1)} %attend_back.2.first_ref), kind=kOutput, calls=%fused_computation.33 | convolution fusion | flops 1611005952 | bytes 6553600 | tf_op jit(solution)/shard_map/dot_general | solution.py:29
  256.5 23.1 %attend_back.3.second_ref = bf16[2048,384]{1,0:T(8,128)(2,1)} custom-call(bf16[2048,768]{1,0:T(8,128)(2,1)} %get-tuple-element.56.q_ref.k_ref.v_ref, bf16[2048,768]{1,0:T(8,128)(2,1)} %get-tuple-element.56.q_ref.k_ref.v_ref, bf16[2048,768]{1,0:T(8,128)(2,1)} %get-tuple-element.56.q_ref.k_ref.v_ref, bf16[2048,256]{1,0:T(8,128)(2,1)} %get-tuple-element.57.o_ref, ...), custom_call_target="tpu_custom_call" | custom-call | flops 10737418240 | bytes 5242880 | tf_op jit(solution)/shard_map/attend_back/pallas_call | solution.py:275
  295.7 3.3 collective-permute-done.26
  303.3 4.5 %convolution_convert_fusion.3 = bf16[1024,384]{1,0:T(8,128)(2,1)S(1)} fusion(bf16[2048,1024]{1,0:T(8,128)(2,1)} %get-tuple-element.62, bf16[2048,384]{1,0:T(8,128)(2,1)S(1)} %copy-done.11), kind=kOutput, calls=%fused_computation.32 | convolution fusion | flops 1611005952 | bytes 6553600 | tf_op jit(solution)/shard_map/dot_general | solution.py:29
  307.8 9.2 %below.1 = bf16[2048,1024]{1,0:T(8,128)(2,1)} custom-call(bf16[2048,384]{1,0:T(8,128)(2,1)} %attend_back.2.first_ref, bf16[2048,384]{1,0:T(8,128)(2,1)} %attend_back.3.second_ref, bf16[1024,768]{1,0:T(8,128)(2,1)} %bitcast.240, f32[1,1024]{1,0:T(1,128)} %get-tuple-element.128.ga_ref.gain_ref, bf16[2048,1024]{1,0:T(8,128)(2,1)} %get-tuple-element.66.term_ref), custom_call_target="tpu_custom_call" | custom-call | flops 3221225472 | bytes 11534336 | tf_op jit(solution)/shard_map/below/pallas_call | solution.py:360
  329.9 7.4 %collective-permute-done.27 = bf16[4,2,2,32,384]{4,3,0,1,2:T(8,128)(2,1)S(1)} collective-permute-done((bf16[4,2,2,32,384]{4,3,0,1,2:T(8,128)(2,1)S(1)}, bf16[4,2,2,32,384]{4,3,0,1,2:T(8,128)(2,1)S(1)}, u32[]{:S(2)}, u32[]{:S(2)}) %collective-permute-start.27) | collective-permute-done | bytes 393248 | tf_op jit(solution)/shard_map/ppermute | solution.py:381
  339.1 5.9 %collective-permute-done.28 = bf16[4,2,32,384]{3,2,0,1:T(8,128)(2,1)S(1)} collective-permute-done((bf16[4,2,32,384]{3,2,0,1:T(8,128)(2,1)S(1)}, bf16[4,2,32,384]{3,2,0,1:T(8,128)(2,1)S(1)}, u32[]{:S(2)}, u32[]{:S(2)}) %collective-permute-start.28) | collective-permute-done | bytes 196640 | tf_op jit(solution)/shard_map/ppermute | solution.py:381
  346.8 5.8 %collective-permute-done.29 = bf16[4,32,384]{2,1,0:T(8,128)(2,1)S(1)} collective-permute-done((bf16[4,32,384]{2,1,0:T(8,128)(2,1)S(1)}, bf16[4,32,384]{2,1,0:T(8,128)(2,1)S(1)}, u32[]{:S(2)}, u32[]{:S(2)}) %collective-permute-start.29) | collective-permute-done | bytes 98336 | tf_op jit(solution)/shard_map/ppermute | solution.py:381
  365.4 16.9 %collective-permute-done.23 = bf16[512,1024]{1,0:T(8,128)(2,1)} collective-permute-done((bf16[512,1024]{1,0:T(8,128)(2,1)}, bf16[512,1024]{1,0:T(8,128)(2,1)}, u32[]{:S(2)}, u32[]{:S(2)}) %collective-permute-start.23) | collective-permute-done | bytes 1048608 | tf_op jit(solution)/shard_map/ppermute | solution.py:381
  384.4 3.5 fusion.15
  (252 shorter events, 99.2 us)
Async XLA Ops:
  7.2 112.7 %all-gather.4.cloned.1.call-start = ((), (), s32[]{:S(2)}) async-start(), calls=%async_computation.1 | async-start | bytes 2359296 | tf_op jit(solution)/shard_map/all_gather | solution.py:488
  7.3 88.1 %collective-permute-start.1 = (bf16[512,1024]{1,0:T(8,128)(2,1)}, bf16[512,1024]{1,0:T(8,128)(2,1)}, u32[]{:S(2)}, u32[]{:S(2)}) collective-permute-start(bf16[512,1024]{1,0:T(8,128)(2,1)} %bitcast.234), channel_id=1, source_target_pairs={{0,16},{8,24},{16,0},{24,8},{1,17},{9,25},{17,1},{25,9},{2,18},{10... | collective-permute-start | bytes 3145736 | tf_op jit(solution)/shard_map/ppermute | solution.py:381
  11.0 23.6 %collective-permute-start.6 = (bf16[2,32]{1,0:T(2,128)(2,1)S(1)}, bf16[2,32]{1,0:T(2,128)(2,1)S(1)}, u32[]{:S(2)}, u32[]{:S(2)}) collective-permute-start(bf16[2,32]{1,0:T(2,128)(2,1)S(1)} %pad_maximum_fusion.13), channel_id=1, source_target_pairs={{0,16},{8,24},{16,0},{24,8},{1,17},{9,25},{17,1},{25,9},{2,18},{10... | collective-permute-start | bytes 392 | tf_op jit(solution)/shard_map/ppermute | solution.py:381
  11.2 84.7 %collective-permute-start.4 = (bf16[512,1024]{1,0:T(8,128)(2,1)}, bf16[512,1024]{1,0:T(8,128)(2,1)}, u32[]{:S(2)}, u32[]{:S(2)}) collective-permute-start(bf16[512,1024]{1,0:T(8,128)(2,1)} %bitcast.253), channel_id=1, source_target_pairs={{0,16},{8,24},{16,0},{24,8},{1,17},{9,25},{17,1},{25,9},{2,18},{10... | collective-permute-start | bytes 3145736 | tf_op jit(solution)/shard_map/ppermute | solution.py:381
  13.1 152.8 %all-gather.6.cloned.1.call-start = ((), (), s32[]{:S(2)}) async-start(), calls=%async_computation.3 | async-start | bytes 2359296 | tf_op jit(solution)/shard_map/all_gather | solution.py:500
  14.9 42.6 %collective-permute-start.13 = (bf16[32,1024]{1,0:T(8,128)(2,1)S(1)}, bf16[32,1024]{1,0:T(8,128)(2,1)S(1)}, u32[]{:S(2)}, u32[]{:S(2)}) collective-permute-start(bf16[32,1024]{1,0:T(8,128)(2,1)S(1)} %bitcast.274), channel_id=1, source_target_pairs={{0,24},{8,16},{16,8},{24,0},{1,25},{9,17},{17,9},{25,1},{2,26},{10... | collective-permute-start | bytes 196616 | tf_op jit(solution)/shard_map/ppermute | solution.py:381
  15.0 44.8 %collective-permute-start.12 = (bf16[32,1024]{1,0:T(8,128)(2,1)S(1)}, bf16[32,1024]{1,0:T(8,128)(2,1)S(1)}, u32[]{:S(2)}, u32[]{:S(2)}) collective-permute-start(bf16[32,1024]{1,0:T(8,128)(2,1)S(1)} %bitcast.273), channel_id=1, source_target_pairs={{0,16},{8,24},{16,0},{24,8},{1,17},{9,25},{17,1},{25,9},{2,18},{10... | collective-permute-start | bytes 196616 | tf_op jit(solution)/shard_map/ppermute | solution.py:381
  35.9 23.9 %collective-permute-start.11 = (bf16[32,1024]{1,0:T(8,128)(2,1)S(1)}, bf16[32,1024]{1,0:T(8,128)(2,1)S(1)}, u32[]{:S(2)}, u32[]{:S(2)}) collective-permute-start(bf16[32,1024]{1,0:T(8,128)(2,1)S(1)} %bitcast.275), channel_id=1, source_target_pairs={{0,8},{8,0},{16,24},{24,16},{1,9},{9,1},{17,25},{25,17},{2,10},{10... | collective-permute-start | bytes 196616 | tf_op jit(solution)/shard_map/ppermute | solution.py:381
  57.5 36.4 %collective-permute-start.19 = (bf16[32,768]{1,0:T(8,128)(2,1)S(1)}, bf16[32,768]{1,0:T(8,128)(2,1)S(1)}, u32[]{:S(2)}, u32[]{:S(2)}) collective-permute-start(bf16[32,768]{1,0:T(8,128)(2,1)S(1)} %get-tuple-element.121), channel_id=1, source_target_pairs={{0,24},{8,16},{16,8},{24,0},{1,25},{9,17},{17,9},{25,1},{2,26},{10... | collective-permute-start | bytes 147464 | tf_op jit(solution)/shard_map/ppermute | solution.py:381
  60.0 13.9 %collective-permute-start.14 = (bf16[4,32,1024]{2,1,0:T(8,128)(2,1)S(1)}, bf16[4,32,1024]{2,1,0:T(8,128)(2,1)S(1)}, u32[]{:S(2)}, u32[]{:S(2)}) collective-permute-start(bf16[4,32,1024]{2,1,0:T(8,128)(2,1)S(1)} %bitcast.260), channel_id=1, source_target_pairs={{0,4},{1,5},{2,6},{3,7},{4,0},{5,1},{6,2},{7,3},{8,12},{9,13},{10,... | collective-permute-start | bytes 786440 | tf_op jit(solution)/shard_map/ppermute | solution.py:381
  74.0 15.2 %collective-permute-start.15 = (bf16[4,2,32,1024]{3,2,1,0:T(8,128)(2,1)S(1)}, bf16[4,2,32,1024]{3,2,1,0:T(8,128)(2,1)S(1)}, u32[]{:S(2)}, u32[]{:S(2)}) collective-permute-start(bf16[4,2,32,1024]{3,2,1,0:T(8,128)(2,1)S(1)} %pad_maximum_fusion.3), channel_id=1, source_target_pairs={{0,2},{1,3},{2,0},{3,1},{4,6},{5,7},{6,4},{7,5},{8,10},{9,11},{10,... | collective-permute-start | bytes 1572872 | tf_op jit(solution)/shard_map/ppermute | solution.py:381
  74.4 12.8 %collective-permute-start.9 = (bf16[2,2,2,2,32]{4,1,0,2,3:T(2,128)(2,1)S(1)}, bf16[2,2,2,2,32]{4,1,0,2,3:T(2,128)(2,1)S(1)}, u32[]{:S(2)}, u32[]{:S(2)}) collective-permute-start(bf16[2,2,2,2,32]{4,1,0,2,3:T(2,128)(2,1)S(1)} %pad_maximum_fusion.10), channel_id=1, source_target_pairs={{0,2},{1,3},{2,0},{3,1},{4,6},{5,7},{6,4},{7,5},{8,10},{9,11},{10,... | collective-permute-start | bytes 3080 | tf_op jit(solution)/shard_map/ppermute | solution.py:381
  93.0 25.2 %collective-permute-start.16 = (bf16[4,2,2,32,1024]{4,3,2,1,0:T(8,128)(2,1)}, bf16[4,2,2,32,1024]{4,3,2,1,0:T(8,128)(2,1)S(1)}, u32[]{:S(2)}, u32[]{:S(2)}) collective-permute-start(bf16[4,2,2,32,1024]{4,3,2,1,0:T(8,128)(2,1)} %pad_maximum_fusion.2), channel_id=1, source_target_pairs={{0,1},{1,0},{2,3},{3,2},{4,5},{5,4},{6,7},{7,6},{8,9},{9,8},{10,11... | collective-permute-start | bytes 3145736 | tf_op jit(solution)/shard_map/ppermute | solution.py:381
  94.6 25.3 %collective-permute-start = (bf16[512,1024]{1,0:T(8,128)(2,1)S(1)}, bf16[512,1024]{1,0:T(8,128)(2,1)}, u32[]{:S(2)}, u32[]{:S(2)}) collective-permute-start(bf16[512,1024]{1,0:T(8,128)(2,1)S(1)} %bitcast.237), channel_id=1, source_target_pairs={{0,8},{8,0},{16,24},{24,16},{1,9},{9,1},{17,25},{25,17},{2,10},{10... | collective-permute-start | bytes 3145736 | tf_op jit(solution)/shard_map/ppermute | solution.py:381
  95.2 24.7 %collective-permute-start.3 = (bf16[512,1024]{1,0:T(8,128)(2,1)}, bf16[512,1024]{1,0:T(8,128)(2,1)}, u32[]{:S(2)}, u32[]{:S(2)}) collective-permute-start(bf16[512,1024]{1,0:T(8,128)(2,1)} %bitcast.254), channel_id=1, source_target_pairs={{0,8},{8,0},{16,24},{24,16},{1,9},{9,1},{17,25},{25,17},{2,10},{10... | collective-permute-start | bytes 3145736 | tf_op jit(solution)/shard_map/ppermute | solution.py:381
  95.4 24.5 %collective-permute-start.2 = (bf16[512,1024]{1,0:T(8,128)(2,1)}, bf16[512,1024]{1,0:T(8,128)(2,1)}, u32[]{:S(2)}, u32[]{:S(2)}) collective-permute-start(bf16[512,1024]{1,0:T(8,128)(2,1)} %collective-permute-done.1.x2), channel_id=1, source_target_pairs={{0,8},{8,0},{16,24},{24,16},{1,9},{9,1},{17,25},{25,17},{2,10},{10... | collective-permute-start | bytes 3145736 | tf_op jit(solution)/shard_map/ppermute | solution.py:381
  95.8 24.1 %collective-permute-start.5 = (bf16[512,1024]{1,0:T(8,128)(2,1)}, bf16[512,1024]{1,0:T(8,128)(2,1)}, u32[]{:S(2)}, u32[]{:S(2)}) collective-permute-start(bf16[512,1024]{1,0:T(8,128)(2,1)} %collective-permute-done.4.g2), channel_id=1, source_target_pairs={{0,8},{8,0},{16,24},{24,16},{1,9},{9,1},{17,25},{25,17},{2,10},{10... | collective-permute-start | bytes 3145736 | tf_op jit(solution)/shard_map/ppermute | solution.py:381
  96.8 206.2 %reduce-scatter.2.cloned.1.call-start = ((), (), s32[]{:S(2)}) async-start(), calls=%async_computation.2 | async-start | bytes 4718592 | tf_op jit(solution)/shard_map/reduce_scatter | solution.py:519
  253.5 45.6 %collective-permute-start.20 = (bf16[2,512,1024]{2,1,0:T(8,128)(2,1)}, bf16[2,512,1024]{2,1,0:T(8,128)(2,1)S(1)}, u32[]{:S(2)}, u32[]{:S(2)}) collective-permute-start(bf16[2,512,1024]{2,1,0:T(8,128)(2,1)} %dynamic-slice_bitcast_fusion.1), channel_id=1, source_target_pairs={{0,8},{8,0},{16,24},{24,16},{1,9},{9,1},{17,25},{25,17},{2,10},{10... | collective-permute-start | bytes 6291464 | tf_op jit(solution)/shard_map/ppermute | solution.py:381
  253.6 29.0 %collective-permute-start.24 = (bf16[4,2,2,32,384]{4,3,2,1,0:T(8,128)(2,1)S(1)}, bf16[4,2,2,32,384]{4,3,2,1,0:T(8,128)(2,1)S(1)}, u32[]{:S(2)}, u32[]{:S(2)}) collective-permute-start(bf16[4,2,2,32,384]{4,3,2,1,0:T(8,128)(2,1)S(1)} %dynamic-slice_bitcast_fusion.4), channel_id=1, source_target_pairs={{0,1},{1,0},{2,3},{3,2},{4,5},{5,4},{6,7},{7,6},{8,9},{9,8},{10,11... | collective-permute-start | bytes 1179656 | tf_op jit(solution)/shard_map/ppermute | solution.py:381
  254.9 24.7 %collective-permute-start.33 = (bf16[2,2,32,1024]{3,2,0,1:T(8,128)(2,1)}, bf16[2,2,32,1024]{3,2,0,1:T(8,128)(2,1)S(1)}, u32[]{:S(2)}, u32[]{:S(2)}) collective-permute-start(bf16[2,2,32,1024]{3,2,0,1:T(8,128)(2,1)} %bitcast.224), channel_id=1, source_target_pairs={{0,1},{1,0},{2,3},{3,2},{4,5},{5,4},{6,7},{7,6},{8,9},{9,8},{10,11... | collective-permute-start | bytes 786440 | tf_op jit(solution)/shard_map/ppermute | solution.py:381
  302.5 81.9 %collective-permute-start.21 = (bf16[512,1024]{1,0:T(8,128)(2,1)}, bf16[512,1024]{1,0:T(8,128)(2,1)}, u32[]{:S(2)}, u32[]{:S(2)}) collective-permute-start(bf16[512,1024]{1,0:T(8,128)(2,1)} %dynamic-slice_bitcast_fusion.3), channel_id=1, source_target_pairs={{0,16},{8,24},{16,0},{24,8},{1,17},{9,25},{17,1},{25,9},{2,18},{10... | collective-permute-start | bytes 3145736 | tf_op jit(solution)/shard_map/ppermute | solution.py:381
  318.9 35.7 %collective-permute-start.22 = (bf16[2,512,1024]{2,1,0:T(8,128)(2,1)S(1)}, bf16[2,512,1024]{2,1,0:T(8,128)(2,1)S(1)}, u32[]{:S(2)}, u32[]{:S(2)}) collective-permute-start(bf16[2,512,1024]{2,1,0:T(8,128)(2,1)S(1)} %dynamic-slice_bitcast_fusion), channel_id=1, source_target_pairs={{0,8},{8,0},{16,24},{24,16},{1,9},{9,1},{17,25},{25,17},{2,10},{10... | collective-permute-start | bytes 6291464 | tf_op jit(solution)/shard_map/ppermute | solution.py:381
  356.7 25.7 %collective-permute-start.23 = (bf16[512,1024]{1,0:T(8,128)(2,1)}, bf16[512,1024]{1,0:T(8,128)(2,1)}, u32[]{:S(2)}, u32[]{:S(2)}) collective-permute-start(bf16[512,1024]{1,0:T(8,128)(2,1)} %dynamic-slice_bitcast_fusion.2), channel_id=1, source_target_pairs={{0,16},{8,24},{16,0},{24,8},{1,17},{9,25},{17,1},{25,9},{2,18},{10... | collective-permute-start | bytes 3145736 | tf_op jit(solution)/shard_map/ppermute | solution.py:381
  (54 other events, 482.1 us)
Sparse Core Ops, SparseCore 0:
  13.2 49.3 all-gather.3
  96.9 51.6 all-gather.5
  168.9 89.2 reduce-scatter.1
where the time goes:
time: 400 us; the launch traced here: 395 us
  waiting for transfers between devices  128 us (32%)
  Pallas kernels  123 us (31%)
  starting transfers between devices  38 us (10%)
  matrix products  35.2 us (9%)
  other arithmetic  31.9 us (8%)
  local copies, waits for them, and re-layouts  24 us (6%)
  between operations  15 us (4%)
    ppermute x39, waiting for transfers between devices, swap(): return lax.ppermute(values, axis, [(i, i ^ bit) for i in range(ways)])  128 us
    pallas_call x2, Pallas kernels, attend_back(): pl.pallas_call(functools.partial(backward_kernel, block), name='attend_ba...  46.5 us
    ppermute x39, starting transfers between devices, swap(): return lax.ppermute(values, axis, [(i, i ^ bit) for i in range(ways)])  37.9 us
    pallas_call x1, Pallas kernels, mlp(): pl.pallas_call(functools.partial(mlp_kernel, count), name='mlp', grid_spe...  28.3 us
    dot_general x5, matrix products, contract_first(): lax.dot_general(left, right, (((0,), (0,)), ((), ())), preferred_element_...  27.4 us
    pallas_call x1, Pallas kernels, attend(): pl.pallas_call(functools.partial(forward_kernel, block), name='attend', g...  26.4 us
    pallas_call x1, Pallas kernels, project(): pl.pallas_call(functools.partial(project_kernel, count), name='project',...  12.3 us
    pallas_call x1, Pallas kernels, below(): pl.pallas_call(below_kernel, name='below', grid=(length // block,), in_sp...  9.21 us
  transfers between devices with their start and end apart: 42, of which 18 were waited for; matrix products, arithmetic and copies ran while one was open for 20% of the time, Pallas kernels for 31%

commit v1 on v0

--- a/solution.py
+++ b/solution.py
@@ -288,6 +288,50 @@
     )(qkv, qkv, qkv, context, grad_context, lse, *tables)
 
 
+def feed_core(normed, upstream, gain, down_ref, up_ref, act_ref, gh_ref):
+    down = down_ref[...]
+    up = up_ref[...]
+    hidden = plain_dot(normed, up)
+    back = contract_last(upstream, down)
+    under = 0.5 + 0.5 * lax.erf(hidden * (0.5**0.5))
+    activated = (hidden * under).astype(BF16)
+    slope = under + hidden * jnp.exp(-0.5 * hidden * hidden) * 0.3989422804014327
+    grad_hidden = (back * slope).astype(BF16)
+    act_ref[...] = activated
+    gh_ref[...] = grad_hidden
+    return plain_dot(activated, down), contract_last(grad_hidden, up) * gain
+
+
+def second_kernel(n_ref, g_ref, part_in, term_in, gain_ref, down_ref, up_ref, act_ref, gh_ref, part_ref, below_ref):
+    part, term = feed_core(n_ref[...], g_ref[...], gain_ref[...], down_ref, up_ref, act_ref, gh_ref)
+    part_ref[...] = (part + part_in[...].astype(F32)).astype(BF16)
+    below_ref[...] = (term + term_in[...].astype(F32)).astype(BF16)
+
+
+def mlp_second(normed, upstream, partial, term, gain_mlp, w_down, w_up, block=256):
+    length, dim = normed.shape
+    hid = w_up.shape[1]
+    whole = lambda i: (0, 0)
+    tile = lambda columns: pl.BlockSpec((block, columns), lambda i: (i, 0))
+    shape = lambda columns: jax.ShapeDtypeStruct((length, columns), BF16)
+    return pl.pallas_call(
+        second_kernel,
+        name="mlp_second",
+        grid=(length // block,),
+        in_specs=[
+            tile(dim), tile(dim), tile(dim), tile(dim),
+            pl.BlockSpec((1, dim), whole),
+            pl.BlockSpec((hid, dim), whole),
+            pl.BlockSpec((dim, hid), whole),
+        ],
+        out_specs=[tile(hid), tile(hid), tile(dim), tile(dim)],
+        out_shape=[shape(hid), shape(hid), shape(dim), shape(dim)],
+        cost_estimate=pl.CostEstimate(
+            flops=8 * length * dim * hid, bytes_accessed=16 * length * dim + 4 * dim * hid, transcendentals=2 * length * hid
+        ),
+    )(normed, upstream, partial, term, gain_mlp, w_down, w_up)
+
+
 def mlp_kernel(
     count, me, x0, x1, x2, x3, g0, g1, g2, g3, gain_ref, down_ref, up_ref,
     n_ref, act_ref, gh_ref, g_ref, part_ref, below_ref, x_held, g_held,
@@ -297,18 +341,9 @@
     n_ref[...] = normed
     upstream = take_piece((g0, g1, g2, g3), g_held, count)
     g_ref[...] = upstream
-    down = down_ref[...]
-    up = up_ref[...]
-    hidden = plain_dot(normed, up)
-    back = contract_last(upstream, down)
-    below = 0.5 + 0.5 * lax.erf(hidden * (0.5**0.5))
-    activated = (hidden * below).astype(BF16)
-    slope = below + hidden * jnp.exp(-0.5 * hidden * hidden) * 0.3989422804014327
-    grad_hidden = (back * slope).astype(BF16)
-    act_ref[...] = activated
-    gh_ref[...] = grad_hidden
-    part_ref[...] = plain_dot(activated, down).astype(BF16)
-    below_ref[...] = (contract_last(grad_hidden, up) * gain).astype(BF16)
+    part, term = feed_core(normed, upstream, gain, down_ref, up_ref, act_ref, gh_ref)
+    part_ref[...] = part.astype(BF16)
+    below_ref[...] = term.astype(BF16)
 
 
 def mlp(me, pieces, grad_pieces, gain_mlp, w_down, w_up, block=256):
@@ -347,8 +382,7 @@
 
 
 def below_kernel(first_ref, second_ref, w_ref, gain_ref, term_ref, o_ref):
-    half = first_ref.shape[1]
-    grad = contract_last(first_ref[...], w_ref[:, :half]) + contract_last(second_ref[...], w_ref[:, half:])
+    grad = contract_last(jnp.concatenate([first_ref[...], second_ref[...]], axis=1), w_ref[...])
     o_ref[...] = (grad * gain_ref[...] + term_ref[...].astype(F32)).astype(BF16)
 
 
@@ -484,10 +518,25 @@
         gather_far_first(jnp.stack([gain_attn, gain_mlp]), "seq", 1), "fsdp", 3
     ).reshape(2, dim).astype(F32)
     down_rows = w_down.shape[0]
-    split_up = w_up.reshape(rows, ways, hid).transpose(1, 0, 2)
-    full_down = lax.all_gather(w_down, "fsdp", tiled=True)
+    half_rows = down_rows // 2
+    half = hid // 2
+    split_up = (
+        w_up.reshape(rows, ways, fold, 2, half_rows).transpose(1, 3, 0, 2, 4).reshape(ways, 2, rows, half)
+    )
     local_up = exchange(split_up, "seq")
-    full_up = gather_far_first(local_up, "fsdp", 1).reshape(dim, hid)
+    local_down = (
+        w_down.reshape(2, 2, rows, 2, half).transpose(0, 3, 1, 2, 4).reshape(2, ways, rows, half)
+    )
+    packed = [jnp.concatenate([local_up[:, k], local_down[k]], axis=1) for k in range(2)]
+    first = lax.all_gather(packed[0], "fsdp")
+    first = first.transpose(1, 0, 2, 3)
+    second = gather_far_first(packed[1], "fsdp", 1).reshape(ways, fold, 2 * rows, half)
+
+    def unpack(both):
+        up = both[:, :, :rows].reshape(dim, half)
+        down = both[:, :, rows:].reshape(2, 2, fold, rows, half).transpose(2, 1, 3, 0, 4)
+        return up, down.reshape(half, dim)
+
     local_rows = layer_input[0]
     row_pieces = gather_sequence(local_rows)
     grad_pieces = gather_sequence(out_grad[0])
@@ -503,17 +552,28 @@
     tables = rotary_tables(length)
     gains, tables = lax.optimization_barrier((gains, tables))
 
+    up_first, down_first = unpack(first)
     normed_mlp, activated, grad_hidden, upstream, partial, mlp_term = mlp(
-        me, row_pieces, grad_pieces, gains[1:2], full_down, full_up
-    )
-    grad_wdown = contract_first(activated, upstream).astype(BF16)
-    grad_wup = contract_first(normed_mlp, grad_hidden).astype(BF16)
+        me, row_pieces, grad_pieces, gains[1:2], down_first, up_first
+    )
+
+    def feed_gradients(activated, grad_hidden):
+        grad_wdown = contract_first(activated, upstream).astype(BF16)
+        grad_wup = contract_first(normed_mlp, grad_hidden).astype(BF16)
+        return (
+            grad_wdown.reshape(fold, half_rows, dim),
+            grad_wup.reshape(ways, fold, rows, half).transpose(1, 0, 2, 3).reshape(fold, ways * rows, half),
+        )
+
+    grads_first = feed_gradients(activated, grad_hidden)
+    up_second, down_second = unpack(second)
+    grads_first, partial = lax.optimization_barrier((grads_first, partial))
+    activated, grad_hidden, partial, mlp_term = mlp_second(
+        normed_mlp, upstream, partial, mlp_term, gains[1:2], down_second, up_second
+    )
+    grads_second = feed_gradients(activated, grad_hidden)
     sendable = jnp.concatenate(
-        [
-            grad_wdown.reshape(fold, down_rows, dim),
-            grad_wup.reshape(ways, fold, rows, hid).transpose(1, 0, 2, 3).reshape(fold, ways * rows, hid),
-        ],
-        axis=1,
+        [grads_first[0], grads_second[0], jnp.concatenate([grads_first[1], grads_second[1]], axis=2)], axis=1
     )
     sendable, full_qkv = lax.optimization_barrier((sendable, full_qkv))
     owned_sum = lax.psum_scatter(sendable, "fsdp", scatter_dimension=0)
@@ -532,8 +592,6 @@
     grad_pairs = []
     for pair in range(count):
         grad_pair = attend_back(qkv, context, grad_context, lse, tables, pair)
-        if pair + 1 == count:
-            grad_pair, owned_sum = lax.optimization_barrier((grad_pair, owned_sum))
         grad_weight = contract_first(normed_attn, grad_pair).astype(BF16)
         if pair + 1 < count:
             grad_weight, grad_context = lax.optimization_barrier((grad_weight, grad_context))
@@ -543,7 +601,9 @@
     upper = below(grad_pairs[0], grad_pairs[1], full_qkv, gains[0:1], mlp_term)
     sum_down = owned_sum[:down_rows].astype(F32)
     back_up = exchange(owned_sum[down_rows:].reshape(ways, rows, hid), "seq")
-    sum_up = back_up.transpose(1, 0, 2).reshape(rows, ways * hid).astype(F32)
+    sum_up = (
+        back_up.reshape(ways, rows, 2, fold, half_rows).transpose(1, 0, 3, 2, 4).reshape(rows, ways * hid).astype(F32)
+    )
     near_qkv = jnp.concatenate(near_pairs, axis=2)
     back_qkv = exchange(near_qkv, "seq")
     sum_qkv = (

time: 400 us -> 449 us (1.12)
  waiting for transfers between devices: 128 us -> 168 us
  local copies, waits for them, and re-layouts: 24 us -> 33.3 us
  Pallas kernels: 123 us -> 128 us
    ppermute x39, waiting for transfers between devices: 128 us -> 167 us  [swap(): return lax.ppermute(values, axis, [(i, i ^ bit) for i in range(ways)])]
    pallas_call x0 -> x1, Pallas kernels: none -> 15.8 us  [mlp_second(): pl.pallas_call(second_kernel, name='mlp_second', grid=(length // block,),...]
    pallas_call x1, Pallas kernels: 28.3 us -> 19 us  [mlp(): pl.pallas_call(functools.partial(mlp_kernel, count), name='mlp', grid_spe...]
    dot_general x5 -> x7, matrix products: 27.4 us -> 24.1 us  [contract_first(): lax.dot_general(left, right, (((0,), (0,)), ((), ())), preferred_element_...]
  transfers between devices with their start and end apart: 42 -> 42, of which waited for: 18 -> 20; matrix products, arithmetic and copies ran while one was open for 20% -> 12% of each run, Pallas kernels for 31% -> 7%
where the time goes in v1:
time: 449 us; the launch traced here: 440 us
  waiting for transfers between devices  168 us (37%)
  Pallas kernels  128 us (29%)
  starting transfers between devices  34.7 us (8%)
  local copies, waits for them, and re-layouts  33.3 us (7%)
  matrix products  32 us (7%)
  other arithmetic  28.9 us (6%)
  between operations  15.1 us (3%)
    ppermute x39, waiting for transfers between devices, swap(): return lax.ppermute(values, axis, [(i, i ^ bit) for i in range(ways)])  167 us
    pallas_call x2, Pallas kernels, attend_back(): pl.pallas_call(functools.partial(backward_kernel, block), name='attend_ba...  46.5 us
    ppermute x39, starting transfers between devices, swap(): return lax.ppermute(values, axis, [(i, i ^ bit) for i in range(ways)])  34.5 us
    pallas_call x1, Pallas kernels, attend(): pl.pallas_call(functools.partial(forward_kernel, block), name='attend', g...  26.7 us
    dot_general x7, matrix products, contract_first(): lax.dot_general(left, right, (((0,), (0,)), ((), ())), preferred_element_...  24.1 us
    pallas_call x1, Pallas kernels, mlp(): pl.pallas_call(functools.partial(mlp_kernel, count), name='mlp', grid_spe...  19 us
    pallas_call x1, Pallas kernels, mlp_second(): pl.pallas_call(second_kernel, name='mlp_second', grid=(length // block,),...  15.8 us
    pallas_call x1, Pallas kernels, project(): pl.pallas_call(functools.partial(project_kernel, count), name='project',...  12.1 us
  transfers between devices with their start and end apart: 42, of which 20 were waited for; matrix products, arithmetic and copies ran while one was open for 12% of the time, Pallas kernels for 7%

profile of v1, /device:TPU:0, one launch (start us, length us, event | category | flops | bytes accessed | tf_op | source)
XLA Modules:
  0.0 440.3 jit_solution(16265788780293425555)
XLA Ops:
  22.1 5.5 %multiply_sine_fusion = (f32[2048,128]{1,0:T(8,128)}, f32[2048,128]{1,0:T(8,128)}) fusion(f32[128]{0:T(128)S(1)} %compare_select_fusion.2, f32[2048]{0:T(1024)S(1)} %iota_convert_fusion), kind=kLoop, calls=%fused_computation.28 | loop fusion | flops 262144 | bytes 2105856 | tf_op jit(solution)/shard_map/sin | solution.py:487
  27.6 15.4 %collective-permute-done.13 = bf16[2,32,512]{2,1,0:T(8,128)(2,1)S(1)} collective-permute-done((bf16[2,32,512]{2,1,0:T(8,128)(2,1)S(1)}, bf16[2,32,512]{2,1,0:T(8,128)(2,1)S(1)}, u32[]{:S(2)}, u32[]{:S(2)}) %collective-permute-start.13) | collective-permute-done | bytes 65568 | tf_op jit(solution)/shard_map/ppermute | solution.py:415
  50.1 24.4 %collective-permute-done.17 = bf16[4,64,512]{2,1,0:T(8,128)(2,1)S(1)} collective-permute-done((bf16[4,64,512]{2,1,0:T(8,128)(2,1)S(1)}, bf16[4,64,512]{2,1,0:T(8,128)(2,1)S(1)}, u32[]{:S(2)}, u32[]{:S(2)}) %collective-permute-start.17) | collective-permute-done | bytes 262176 | tf_op jit(solution)/shard_map/ppermute | solution.py:415
  77.3 10.9 %collective-permute-done.18 = bf16[4,2,64,512]{3,2,0,1:T(8,128)(2,1)S(1)} collective-permute-done((bf16[4,2,64,512]{3,2,0,1:T(8,128)(2,1)S(1)}, bf16[4,2,64,512]{3,2,0,1:T(8,128)(2,1)S(1)}, u32[]{:S(2)}, u32[]{:S(2)}) %collective-permute-start.18) | collective-permute-done | bytes 524320 | tf_op jit(solution)/shard_map/ppermute | solution.py:415
  95.3 26.9 %collective-permute-done.10 = bf16[2,2,2,2,2,32]{5,1,0,2,3,4:T(2,128)(2,1)S(1)} collective-permute-done((bf16[2,2,2,2,2,32]{5,1,0,2,3,4:T(2,128)(2,1)S(1)}, bf16[2,2,2,2,2,32]{5,1,0,2,3,4:T(2,128)(2,1)S(1)}, u32[]{:S(2)}, u32[]{:S(2)}) %collective-permute-start.10) | collective-permute-done | bytes 2080 | tf_op jit(solution)/shard_map/ppermute | solution.py:415
  139.7 19.0 %mlp.1 = (bf16[2048,1024]{1,0:T(8,128)(2,1)}, bf16[2048,512]{1,0:T(8,128)(2,1)}, bf16[2048,512]{1,0:T(8,128)(2,1)}, bf16[2048,1024]{1,0:T(8,128)(2,1)}, bf16[204...) custom-call(s32[1]{0:T(128)} %bitcast.1.me, bf16[512,1024]{1,0:T(8,128)(2,1)} %bitcast.258, ...), custom_call_target="tpu_custom_call" | custom-call | flops 8589934592 | bytes 35651584 | tf_op jit(solution)/shard_map/mlp/pallas_call | solution.py:358
  158.7 5.4 %convolution_convert_fusion.3 = bf16[1024,512]{1,0:T(8,128)(2,1)S(1)} fusion(bf16[2048,1024]{1,0:T(8,128)(2,1)} %get-tuple-element.56.n_ref, bf16[2048,512]{1,0:T(8,128)(2,1)} %get-tuple-element.57), kind=kOutput, calls=%fused_computation.32 | convolution fusion | flops 2148007936 | bytes 7340032 | tf_op jit(solution)/shard_map/dot_general | solution.py:29
  168.0 15.8 %mlp_second.1 = (bf16[2048,512]{1,0:T(8,128)(2,1)}, bf16[2048,512]{1,0:T(8,128)(2,1)}, bf16[2048,1024]{1,0:T(8,128)(2,1)}, bf16[2048,1024]{1,0:T(8,128)(2,1)}) custom-call(bf16[2048,1024]{1,0:T(8,128)(2,1)} %get-tuple-element.56.n_ref, bf16[2048,1024]{1,0:T(8,128)(2,1)} %get-tuple-element.54.g_ref, bf16[2048,1024]{1,0:T(8,128)(2,1)} %get-tuple-element.60.part_in, ...), custom_call_target="tpu_custom_call" | custom-call | flops 8589934592 | bytes 35651584 | tf_op jit(solution)/shard_map/mlp_second/pallas_call | solution.py:317
  183.8 5.4 %convolution_convert_fusion.1 = bf16[1024,512]{1,0:T(8,128)(2,1)S(1)} fusion(bf16[2048,1024]{1,0:T(8,128)(2,1)} %get-tuple-element.56.n_ref, bf16[2048,512]{1,0:T(8,128)(2,1)} %get-tuple-element.64), kind=kOutput, calls=%fused_computation.30 | convolution fusion | flops 2148007936 | bytes 7340032 | tf_op jit(solution)/shard_map/dot_general | solution.py:29
  195.4 12.1 %project.1 = (bf16[2048,1024]{1,0:T(8,128)(2,1)}, bf16[2048,768]{1,0:T(8,128)(2,1)}) custom-call(s32[1]{0:T(128)} %bitcast.1.me, bf16[512,1024]{1,0:T(8,128)(2,1)} %bitcast.259, bf16[512,1024]{1,0:T(8,128)(2,1)} %collective-permute-done.x1, bf16[512,1024]{1,0:T(8,128)(2,1)} %collective-permute-done.1.x2, bf16[512,1024]{1,0:T(8,128)(2,1)} %collective-permute-done.2.x3, ...), custom_call_target="tpu_custom_call" | custom-call | flops 3221225472 | bytes 15728640 | tf_op jit(solution)/shard_map/project/pallas_call | solution.py:101
  207.5 26.7 %attend.1 = (bf16[2048,256]{1,0:T(8,128)(2,1)}, f32[2048,256]{1,0:T(8,128)}) custom-call(bf16[2048,768]{1,0:T(8,128)(2,1)} %get-tuple-element.68.q_ref.k_ref.v_ref, bf16[2048,768]{1,0:T(8,128)(2,1)} %get-tuple-element.68.q_ref.k_ref.v_ref, bf16[2048,768]{1,0:T(8,128)(2,1)} %get-tuple-element.68.q_ref.k_ref.v_ref), custom_call_target="tpu_custom_call" | custom-call | flops 8589934592 | bytes 6291456 | tf_op jit(solution)/shard_map/attend/pallas_call | solution.py:182
  234.2 4.6 %convolution_convert_fusion.do_ref = bf16[2048,256]{1,0:T(8,128)(2,1)} fusion(bf16[2048,1024]{1,0:T(8,128)(2,1)} %get-tuple-element.54.g_ref, bf16[256,1024]{1,0:T(8,128)(2,1)S(1)} %bitcast.272), kind=kOutput, calls=%fused_computation.9 | convolution fusion | flops 1074266112 | bytes 5767168 | tf_op jit(solution)/shard_map/dot_general | solution.py:25
  244.3 23.4 %attend_back.2.first_ref = bf16[2048,384]{1,0:T(8,128)(2,1)} custom-call(bf16[2048,768]{1,0:T(8,128)(2,1)} %get-tuple-element.68.q_ref.k_ref.v_ref, bf16[2048,768]{1,0:T(8,128)(2,1)} %get-tuple-element.68.q_ref.k_ref.v_ref, bf16[2048,768]{1,0:T(8,128)(2,1)} %get-tuple-element.68.q_ref.k_ref.v_ref, bf16[2048,256]{1,0:T(8,128)(2,1)} %get-tuple-element.69.o_ref, ...), custom_call_target="tpu_custom_call" | custom-call | flops 10737418240 | bytes 5242880 | tf_op jit(solution)/shard_map/attend_back/pallas_call | solution.py:275
  267.7 5.0 %convolution_convert_fusion.6 = bf16[1024,384]{1,0:T(8,128)(2,1)S(1)} fusion(bf16[2048,1024]{1,0:T(8,128)(2,1)} %get-tuple-element.74, bf16[2048,384]{1,0:T(8,128)(2,1)} %attend_back.2.first_ref), kind=kOutput, calls=%fused_computation.35 | convolution fusion | flops 1611005952 | bytes 6553600 | tf_op jit(solution)/shard_map/dot_general | solution.py:29
  272.8 23.1 %attend_back.3.second_ref = bf16[2048,384]{1,0:T(8,128)(2,1)} custom-call(bf16[2048,768]{1,0:T(8,128)(2,1)} %get-tuple-element.68.q_ref.k_ref.v_ref, bf16[2048,768]{1,0:T(8,128)(2,1)} %get-tuple-element.68.q_ref.k_ref.v_ref, bf16[2048,768]{1,0:T(8,128)(2,1)} %get-tuple-element.68.q_ref.k_ref.v_ref, bf16[2048,256]{1,0:T(8,128)(2,1)} %get-tuple-element.69.o_ref, ...), custom_call_target="tpu_custom_call" | custom-call | flops 10737418240 | bytes 5242880 | tf_op jit(solution)/shard_map/attend_back/pallas_call | solution.py:275
  295.8 8.5 %below.1 = bf16[2048,1024]{1,0:T(8,128)(2,1)} custom-call(bf16[2048,384]{1,0:T(8,128)(2,1)} %attend_back.2.first_ref, bf16[2048,384]{1,0:T(8,128)(2,1)} %attend_back.3.second_ref, bf16[1024,768]{1,0:T(8,128)(2,1)} %bitcast.264, f32[1,1024]{1,0:T(1,128)} %get-tuple-element.146.ga_ref.gain_ref, bf16[2048,1024]{1,0:T(8,128)(2,1)} %get-tuple-element.76.term_ref), custom_call_target="tpu_custom_call" | custom-call | flops 3221225472 | bytes 11534336 | tf_op jit(solution)/shard_map/below/pallas_call | solution.py:394
  314.7 4.0 collective-permute-done.33
  319.6 10.9 %collective-permute-done.24 = bf16[4,2,2,32,384]{4,3,2,1,0:T(8,128)(2,1)S(1)} collective-permute-done((bf16[4,2,2,32,384]{4,3,2,1,0:T(8,128)(2,1)S(1)}, bf16[4,2,2,32,384]{4,3,2,1,0:T(8,128)(2,1)S(1)}, u32[]{:S(2)}, u32[]{:S(2)}) %collective-permute-start.24) | collective-permute-done | bytes 393248 | tf_op jit(solution)/shard_map/ppermute | solution.py:415
  332.0 11.3 %collective-permute-done.27 = bf16[4,2,2,32,384]{4,3,0,1,2:T(8,128)(2,1)S(1)} collective-permute-done((bf16[4,2,2,32,384]{4,3,0,1,2:T(8,128)(2,1)S(1)}, bf16[4,2,2,32,384]{4,3,0,1,2:T(8,128)(2,1)S(1)}, u32[]{:S(2)}, u32[]{:S(2)}) %collective-permute-start.27) | collective-permute-done | bytes 393248 | tf_op jit(solution)/shard_map/ppermute | solution.py:415
  348.2 5.0 %collective-permute-done.28 = bf16[4,2,32,384]{3,2,0,1:T(8,128)(2,1)S(1)} collective-permute-done((bf16[4,2,32,384]{3,2,0,1:T(8,128)(2,1)S(1)}, bf16[4,2,32,384]{3,2,0,1:T(8,128)(2,1)S(1)}, u32[]{:S(2)}, u32[]{:S(2)}) %collective-permute-start.28) | collective-permute-done | bytes 196640 | tf_op jit(solution)/shard_map/ppermute | solution.py:415
  353.4 5.3 %collective-permute-done.26 = bf16[4,32,384]{2,1,0:T(8,128)(2,1)S(1)} collective-permute-done((bf16[4,32,384]{2,1,0:T(8,128)(2,1)S(1)}, bf16[4,32,384]{2,1,0:T(8,128)(2,1)S(1)}, u32[]{:S(2)}, u32[]{:S(2)}) %collective-permute-start.26) | collective-permute-done | bytes 98336 | tf_op jit(solution)/shard_map/ppermute | solution.py:415
  358.8 6.5 %collective-permute-done.29 = bf16[4,32,384]{2,1,0:T(8,128)(2,1)S(1)} collective-permute-done((bf16[4,32,384]{2,1,0:T(8,128)(2,1)S(1)}, bf16[4,32,384]{2,1,0:T(8,128)(2,1)S(1)}, u32[]{:S(2)}, u32[]{:S(2)}) %collective-permute-start.29) | collective-permute-done | bytes 98336 | tf_op jit(solution)/shard_map/ppermute | solution.py:415
  383.5 15.3 %collective-permute-done.23 = bf16[512,1024]{1,0:T(8,128)(2,1)S(1)} collective-permute-done((bf16[512,1024]{1,0:T(8,128)(2,1)}, bf16[512,1024]{1,0:T(8,128)(2,1)S(1)}, u32[]{:S(2)}, u32[]{:S(2)}) %collective-permute-start.23) | collective-permute-done | bytes 1048608 | tf_op jit(solution)/shard_map/ppermute | solution.py:415
  399.7 21.0 %collective-permute-done.21 = bf16[512,1024]{1,0:T(8,128)(2,1)S(1)} collective-permute-done((bf16[512,1024]{1,0:T(8,128)(2,1)S(1)}, bf16[512,1024]{1,0:T(8,128)(2,1)S(1)}, u32[]{:S(2)}, u32[]{:S(2)}) %collective-permute-start.21) | collective-permute-done | bytes 1048608 | tf_op jit(solution)/shard_map/ppermute | solution.py:415
  (268 shorter events, 113.9 us)
Async XLA Ops:
  7.2 121.8 %all-gather.7.cloned.1.call-start = ((), (), s32[]{:S(2)}) async-start(), calls=%async_computation.3 | async-start | bytes 2359296 | tf_op jit(solution)/shard_map/all_gather | solution.py:549
  16.5 118.0 %all-gather.5.cloned.1.call-start = ((), (), s32[]{:S(2)}) async-start(), calls=%async_computation.2 | async-start | bytes 2359296 | tf_op jit(solution)/shard_map/all_gather | solution.py:531
  16.5 123.2 %collective-permute-start = (bf16[512,1024]{1,0:T(8,128)(2,1)S(1)}, bf16[512,1024]{1,0:T(8,128)(2,1)}, u32[]{:S(2)}, u32[]{:S(2)}) collective-permute-start(bf16[512,1024]{1,0:T(8,128)(2,1)S(1)} %bitcast.260), channel_id=1, source_target_pairs={{0,8},{8,0},{16,24},{24,16},{1,9},{9,1},{17,25},{25,17},{2,10},{10... | collective-permute-start | bytes 3145736 | tf_op jit(solution)/shard_map/ppermute | solution.py:415
  16.6 106.4 %collective-permute-start.1 = (bf16[512,1024]{1,0:T(8,128)(2,1)S(1)}, bf16[512,1024]{1,0:T(8,128)(2,1)}, u32[]{:S(2)}, u32[]{:S(2)}) collective-permute-start(bf16[512,1024]{1,0:T(8,128)(2,1)S(1)} %bitcast.261), channel_id=1, source_target_pairs={{0,16},{8,24},{16,0},{24,8},{1,17},{9,25},{17,1},{25,9},{2,18},{10... | collective-permute-start | bytes 3145736 | tf_op jit(solution)/shard_map/ppermute | solution.py:415
  19.0 24.0 %collective-permute-start.13 = (bf16[2,32,512]{2,1,0:T(8,128)(2,1)S(1)}, bf16[2,32,512]{2,1,0:T(8,128)(2,1)S(1)}, u32[]{:S(2)}, u32[]{:S(2)}) collective-permute-start(bf16[2,32,512]{2,1,0:T(8,128)(2,1)S(1)} %get-tuple-element.131), channel_id=1, source_target_pairs={{0,24},{8,16},{16,8},{24,0},{1,25},{9,17},{17,9},{25,1},{2,26},{10... | collective-permute-start | bytes 196616 | tf_op jit(solution)/shard_map/ppermute | solution.py:415
  19.5 25.5 %collective-permute-start.12 = (bf16[2,32,512]{2,1,0:T(8,128)(2,1)S(1)}, bf16[2,32,512]{2,1,0:T(8,128)(2,1)S(1)}, u32[]{:S(2)}, u32[]{:S(2)}) collective-permute-start(bf16[2,32,512]{2,1,0:T(8,128)(2,1)S(1)} %get-tuple-element.132), channel_id=1, source_target_pairs={{0,16},{8,24},{16,0},{24,8},{1,17},{9,25},{17,1},{25,9},{2,18},{10... | collective-permute-start | bytes 196616 | tf_op jit(solution)/shard_map/ppermute | solution.py:415
  20.9 25.5 %collective-permute-start.11 = (bf16[2,32,512]{2,1,0:T(8,128)(2,1)S(1)}, bf16[2,32,512]{2,1,0:T(8,128)(2,1)S(1)}, u32[]{:S(2)}, u32[]{:S(2)}) collective-permute-start(bf16[2,32,512]{2,1,0:T(8,128)(2,1)S(1)} %get-tuple-element.133), channel_id=1, source_target_pairs={{0,8},{8,0},{16,24},{24,16},{1,9},{9,1},{17,25},{25,17},{2,10},{10... | collective-permute-start | bytes 196616 | tf_op jit(solution)/shard_map/ppermute | solution.py:415
  45.0 78.5 %collective-permute-start.4 = (bf16[512,1024]{1,0:T(8,128)(2,1)S(1)}, bf16[512,1024]{1,0:T(8,128)(2,1)}, u32[]{:S(2)}, u32[]{:S(2)}) collective-permute-start(bf16[512,1024]{1,0:T(8,128)(2,1)S(1)} %bitcast.283), channel_id=1, source_target_pairs={{0,16},{8,24},{16,0},{24,8},{1,17},{9,25},{17,1},{25,9},{2,18},{10... | collective-permute-start | bytes 3145736 | tf_op jit(solution)/shard_map/ppermute | solution.py:415
  46.6 28.0 %collective-permute-start.17 = (bf16[4,64,512]{2,1,0:T(8,128)(2,1)S(1)}, bf16[4,64,512]{2,1,0:T(8,128)(2,1)S(1)}, u32[]{:S(2)}, u32[]{:S(2)}) collective-permute-start(bf16[4,64,512]{2,1,0:T(8,128)(2,1)S(1)} %pad_maximum_fusion.6), channel_id=1, source_target_pairs={{0,4},{1,5},{2,6},{3,7},{4,0},{5,1},{6,2},{7,3},{8,12},{9,13},{10,... | collective-permute-start | bytes 786440 | tf_op jit(solution)/shard_map/ppermute | solution.py:415
  49.2 25.5 %collective-permute-start.7 = (bf16[2,2,32]{2,0,1:T(2,128)(2,1)S(1)}, bf16[2,2,32]{2,0,1:T(2,128)(2,1)S(1)}, u32[]{:S(2)}, u32[]{:S(2)}) collective-permute-start(bf16[2,2,32]{2,0,1:T(2,128)(2,1)S(1)} %pad_maximum_fusion.13), channel_id=1, source_target_pairs={{0,8},{8,0},{16,24},{24,16},{1,9},{9,1},{17,25},{25,17},{2,10},{10... | collective-permute-start | bytes 776 | tf_op jit(solution)/shard_map/ppermute | solution.py:415
  50.1 373.1 %reduce-scatter.2.cloned.1.call-start = ((), (), s32[]{:S(2)}) async-start(), calls=%async_computation.1 | async-start | bytes 4718592 | tf_op jit(solution)/shard_map/reduce_scatter | solution.py:579
  89.4 34.2 %collective-permute-start.19 = (bf16[4,2,2,64,512]{4,3,0,1,2:T(8,128)(2,1)}, bf16[4,2,2,64,512]{4,3,0,1,2:T(8,128)(2,1)}, u32[]{:S(2)}, u32[]{:S(2)}) collective-permute-start(bf16[4,2,2,64,512]{4,3,0,1,2:T(8,128)(2,1)} %pad_maximum_fusion.1), channel_id=1, source_target_pairs={{0,1},{1,0},{2,3},{3,2},{4,5},{5,4},{6,7},{7,6},{8,9},{9,8},{10,11... | collective-permute-start | bytes 3145736 | tf_op jit(solution)/shard_map/ppermute | solution.py:415
  94.6 27.6 %collective-permute-start.10 = (bf16[2,2,2,2,2,32]{5,1,0,2,3,4:T(2,128)(2,1)S(1)}, bf16[2,2,2,2,2,32]{5,1,0,2,3,4:T(2,128)(2,1)S(1)}, u32[]{:S(2)}, u32[]{:S(2)}) collective-permute-start(bf16[2,2,2,2,2,32]{5,1,0,2,3,4:T(2,128)(2,1)S(1)} %pad_maximum_fusion.10), channel_id=1, source_target_pairs={{0,1},{1,0},{2,3},{3,2},{4,5},{5,4},{6,7},{7,6},{8,9},{9,8},{10,11... | collective-permute-start | bytes 6152 | tf_op jit(solution)/shard_map/ppermute | solution.py:415
  122.2 17.5 %collective-permute-start.3 = (bf16[512,1024]{1,0:T(8,128)(2,1)S(1)}, bf16[512,1024]{1,0:T(8,128)(2,1)}, u32[]{:S(2)}, u32[]{:S(2)}) collective-permute-start(bf16[512,1024]{1,0:T(8,128)(2,1)S(1)} %bitcast.284), channel_id=1, source_target_pairs={{0,8},{8,0},{16,24},{24,16},{1,9},{9,1},{17,25},{25,17},{2,10},{10... | collective-permute-start | bytes 3145736 | tf_op jit(solution)/shard_map/ppermute | solution.py:415
  123.0 16.7 %collective-permute-start.2 = (bf16[512,1024]{1,0:T(8,128)(2,1)}, bf16[512,1024]{1,0:T(8,128)(2,1)}, u32[]{:S(2)}, u32[]{:S(2)}) collective-permute-start(bf16[512,1024]{1,0:T(8,128)(2,1)} %collective-permute-done.1.x2), channel_id=1, source_target_pairs={{0,8},{8,0},{16,24},{24,16},{1,9},{9,1},{17,25},{25,17},{2,10},{10... | collective-permute-start | bytes 3145736 | tf_op jit(solution)/shard_map/ppermute | solution.py:415
  123.5 16.2 %collective-permute-start.5 = (bf16[512,1024]{1,0:T(8,128)(2,1)}, bf16[512,1024]{1,0:T(8,128)(2,1)}, u32[]{:S(2)}, u32[]{:S(2)}) collective-permute-start(bf16[512,1024]{1,0:T(8,128)(2,1)} %collective-permute-done.4.g2), channel_id=1, source_target_pairs={{0,8},{8,0},{16,24},{24,16},{1,9},{9,1},{17,25},{25,17},{2,10},{10... | collective-permute-start | bytes 3145736 | tf_op jit(solution)/shard_map/ppermute | solution.py:415
  306.3 64.3 %collective-permute-start.22 = (bf16[2,512,1024]{2,1,0:T(8,128)(2,1)S(1)}, bf16[2,512,1024]{2,1,0:T(8,128)(2,1)S(1)}, u32[]{:S(2)}, u32[]{:S(2)}) collective-permute-start(bf16[2,512,1024]{2,1,0:T(8,128)(2,1)S(1)} %dynamic-slice_bitcast_fusion), channel_id=1, source_target_pairs={{0,8},{8,0},{16,24},{24,16},{1,9},{9,1},{17,25},{25,17},{2,10},{10... | collective-permute-start | bytes 6291464 | tf_op jit(solution)/shard_map/ppermute | solution.py:415
  312.3 64.8 %collective-permute-start.20 = (bf16[2,512,1024]{2,1,0:T(8,128)(2,1)}, bf16[2,512,1024]{2,1,0:T(8,128)(2,1)}, u32[]{:S(2)}, u32[]{:S(2)}) collective-permute-start(bf16[2,512,1024]{2,1,0:T(8,128)(2,1)} %dynamic-slice_bitcast_fusion.1), channel_id=1, source_target_pairs={{0,8},{8,0},{16,24},{24,16},{1,9},{9,1},{17,25},{25,17},{2,10},{10... | collective-permute-start | bytes 6291464 | tf_op jit(solution)/shard_map/ppermute | solution.py:415
  312.4 18.1 %collective-permute-start.24 = (bf16[4,2,2,32,384]{4,3,2,1,0:T(8,128)(2,1)S(1)}, bf16[4,2,2,32,384]{4,3,2,1,0:T(8,128)(2,1)S(1)}, u32[]{:S(2)}, u32[]{:S(2)}) collective-permute-start(bf16[4,2,2,32,384]{4,3,2,1,0:T(8,128)(2,1)S(1)} %dynamic-slice_bitcast_fusion.4), channel_id=1, source_target_pairs={{0,1},{1,0},{2,3},{3,2},{4,5},{5,4},{6,7},{7,6},{8,9},{9,8},{10,11... | collective-permute-start | bytes 1179656 | tf_op jit(solution)/shard_map/ppermute | solution.py:415
  313.8 29.5 %collective-permute-start.27 = (bf16[4,2,2,32,384]{4,3,0,1,2:T(8,128)(2,1)S(1)}, bf16[4,2,2,32,384]{4,3,0,1,2:T(8,128)(2,1)S(1)}, u32[]{:S(2)}, u32[]{:S(2)}) collective-permute-start(bf16[4,2,2,32,384]{4,3,0,1,2:T(8,128)(2,1)S(1)} %bitcast.307), channel_id=1, source_target_pairs={{0,1},{1,0},{2,3},{3,2},{4,5},{5,4},{6,7},{7,6},{8,9},{9,8},{10,11... | collective-permute-start | bytes 1179656 | tf_op jit(solution)/shard_map/ppermute | solution.py:415
  318.7 26.2 %collective-permute-start.34 = (bf16[2,32,1024]{2,1,0:T(8,128)(2,1)S(1)}, bf16[2,32,1024]{2,1,0:T(8,128)(2,1)S(1)}, u32[]{:S(2)}, u32[]{:S(2)}) collective-permute-start(bf16[2,32,1024]{2,1,0:T(8,128)(2,1)S(1)} %dynamic-slice_bitcast_fusion.7), channel_id=1, source_target_pairs={{0,2},{1,3},{2,0},{3,1},{4,6},{5,7},{6,4},{7,5},{8,10},{9,11},{10,... | collective-permute-start | bytes 393224 | tf_op jit(solution)/shard_map/ppermute | solution.py:415
  345.1 22.0 %collective-permute-start.35 = (bf16[32,1024]{1,0:T(8,128)(2,1)S(1)}, bf16[32,1024]{1,0:T(8,128)(2,1)S(1)}, u32[]{:S(2)}, u32[]{:S(2)}) collective-permute-start(bf16[32,1024]{1,0:T(8,128)(2,1)S(1)} %dynamic-slice_bitcast_fusion.13), channel_id=1, source_target_pairs={{0,4},{1,5},{2,6},{3,7},{4,0},{5,1},{6,2},{7,3},{8,12},{9,13},{10,... | collective-permute-start | bytes 196616 | tf_op jit(solution)/shard_map/ppermute | solution.py:415
  372.6 26.2 %collective-permute-start.23 = (bf16[512,1024]{1,0:T(8,128)(2,1)}, bf16[512,1024]{1,0:T(8,128)(2,1)S(1)}, u32[]{:S(2)}, u32[]{:S(2)}) collective-permute-start(bf16[512,1024]{1,0:T(8,128)(2,1)} %dynamic-slice_bitcast_fusion.2), channel_id=1, source_target_pairs={{0,16},{8,24},{16,0},{24,8},{1,17},{9,25},{17,1},{25,9},{2,18},{10... | collective-permute-start | bytes 3145736 | tf_op jit(solution)/shard_map/ppermute | solution.py:415
  380.6 40.2 %collective-permute-start.21 = (bf16[512,1024]{1,0:T(8,128)(2,1)S(1)}, bf16[512,1024]{1,0:T(8,128)(2,1)S(1)}, u32[]{:S(2)}, u32[]{:S(2)}) collective-permute-start(bf16[512,1024]{1,0:T(8,128)(2,1)S(1)} %dynamic-slice_bitcast_fusion.3), channel_id=1, source_target_pairs={{0,16},{8,24},{16,0},{24,8},{1,17},{9,25},{17,1},{25,9},{2,18},{10... | collective-permute-start | bytes 3145736 | tf_op jit(solution)/shard_map/ppermute | solution.py:415
  (53 other events, 441.9 us)
Sparse Core Ops, SparseCore 0:
  16.6 59.3 all-gather.6
  78.7 55.6 all-gather.4
  272.9 104.0 reduce-scatter.1

commit v2 on v1

--- a/solution.py
+++ b/solution.py
@@ -288,6 +288,26 @@
     )(qkv, qkv, qkv, context, grad_context, lse, *tables)
 
 
+def unpack(up_ref, down_ref, up_held, down_held, fold_first):
+    lead, second, rows, half = up_ref.shape
+    fold, ways = (lead, second) if fold_first else (second, lead)
+    for f in range(fold):
+        for k in range(ways):
+            source = (f, k) if fold_first else (k, f)
+            at = (k * fold + f) * rows
+            up_held[at : at + rows, :] = up_ref[source]
+            at = (f * 2 + k % 2) * rows
+            down_held[at : at + rows, (k // 2) * half : (k // 2 + 1) * half] = down_ref[source]
+
+
+def packed_specs(packed):
+    shape = (packed.shape[0], packed.shape[1], packed.shape[2] // 2, packed.shape[3])
+    return [
+        pl.BlockSpec(shape, lambda i, *_: (0, 0, 0, 0)),
+        pl.BlockSpec(shape, lambda i, *_: (0, 0, 1, 0)),
+    ]
+
+
 def feed_core(normed, upstream, gain, down_ref, up_ref, act_ref, gh_ref):
     down = down_ref[...]
     up = up_ref[...]
@@ -302,15 +322,22 @@
     return plain_dot(activated, down), contract_last(grad_hidden, up) * gain
 
 
-def second_kernel(n_ref, g_ref, part_in, term_in, gain_ref, down_ref, up_ref, act_ref, gh_ref, part_ref, below_ref):
-    part, term = feed_core(n_ref[...], g_ref[...], gain_ref[...], down_ref, up_ref, act_ref, gh_ref)
+def second_kernel(
+    n_ref, g_ref, part_in, term_in, gain_ref, up_ref, down_ref,
+    act_ref, gh_ref, part_ref, below_ref, up_held, down_held,
+):
+    @pl.when(pl.program_id(0) == 0)
+    def _():
+        unpack(up_ref, down_ref, up_held, down_held, False)
+
+    part, term = feed_core(n_ref[...], g_ref[...], gain_ref[...], down_held, up_held, act_ref, gh_ref)
     part_ref[...] = (part + part_in[...].astype(F32)).astype(BF16)
     below_ref[...] = (term + term_in[...].astype(F32)).astype(BF16)
 
 
-def mlp_second(normed, upstream, partial, term, gain_mlp, w_down, w_up, block=256):
+def mlp_second(normed, upstream, partial, term, gain_mlp, packed, block=256):
     length, dim = normed.shape
-    hid = w_up.shape[1]
+    hid = packed.shape[3]
     whole = lambda i: (0, 0)
     tile = lambda columns: pl.BlockSpec((block, columns), lambda i: (i, 0))
     shape = lambda columns: jax.ShapeDtypeStruct((length, columns), BF16)
@@ -321,35 +348,39 @@
         in_specs=[
             tile(dim), tile(dim), tile(dim), tile(dim),
             pl.BlockSpec((1, dim), whole),
-            pl.BlockSpec((hid, dim), whole),
-            pl.BlockSpec((dim, hid), whole),
-        ],
+        ]
+        + packed_specs(packed),
         out_specs=[tile(hid), tile(hid), tile(dim), tile(dim)],
+        scratch_shapes=[pltpu.VMEM((dim, hid), BF16), pltpu.VMEM((hid, dim), BF16)],
         out_shape=[shape(hid), shape(hid), shape(dim), shape(dim)],
         cost_estimate=pl.CostEstimate(
             flops=8 * length * dim * hid, bytes_accessed=16 * length * dim + 4 * dim * hid, transcendentals=2 * length * hid
         ),
-    )(normed, upstream, partial, term, gain_mlp, w_down, w_up)
+    )(normed, upstream, partial, term, gain_mlp, packed, packed)
 
 
 def mlp_kernel(
-    count, me, x0, x1, x2, x3, g0, g1, g2, g3, gain_ref, down_ref, up_ref,
-    n_ref, act_ref, gh_ref, g_ref, part_ref, below_ref, x_held, g_held,
+    count, me, x0, x1, x2, x3, g0, g1, g2, g3, gain_ref, up_ref, down_ref,
+    n_ref, act_ref, gh_ref, g_ref, part_ref, below_ref, x_held, g_held, up_held, down_held,
 ):
+    @pl.when(pl.program_id(0) == 0)
+    def _():
+        unpack(up_ref, down_ref, up_held, down_held, True)
+
     gain = gain_ref[...]
     normed = normalize(take_piece((x0, x1, x2, x3), x_held, count).astype(F32), gain)
     n_ref[...] = normed
     upstream = take_piece((g0, g1, g2, g3), g_held, count)
     g_ref[...] = upstream
-    part, term = feed_core(normed, upstream, gain, down_ref, up_ref, act_ref, gh_ref)
+    part, term = feed_core(normed, upstream, gain, down_held, up_held, act_ref, gh_ref)
     part_ref[...] = part.astype(BF16)
     below_ref[...] = term.astype(BF16)
 
 
-def mlp(me, pieces, grad_pieces, gain_mlp, w_down, w_up, block=256):
+def mlp(me, pieces, grad_pieces, gain_mlp, packed, block=256):
     tokens, dim = pieces[0].shape
     length = 4 * tokens
-    hid = w_up.shape[1]
+    hid = packed.shape[3]
     count = tokens // block
     whole = lambda i, me: (0, 0)
     part = lambda i, me: (place(i, me, count), 0)
@@ -365,49 +396,54 @@
             + piece_specs(grad_pieces, block)
             + [
                 pl.BlockSpec((1, dim), whole),
-                pl.BlockSpec((hid, dim), whole),
-                pl.BlockSpec((dim, hid), whole),
-            ],
+            ]
+            + packed_specs(packed),
             out_specs=[tile(dim), tile(hid), tile(hid), tile(dim), tile(dim), tile(dim)],
             scratch_shapes=[
                 pltpu.VMEM((block, dim), BF16),
                 pltpu.VMEM((block, dim), BF16),
+                pltpu.VMEM((dim, hid), BF16),
+                pltpu.VMEM((hid, dim), BF16),
             ],
         ),
         out_shape=[shape(dim), shape(hid), shape(hid), shape(dim), shape(dim), shape(dim)],
         cost_estimate=pl.CostEstimate(
             flops=8 * length * dim * hid, bytes_accessed=16 * length * dim + 4 * dim * hid, transcendentals=2 * length * hid
         ),
-    )(me, *pieces, *grad_pieces, gain_mlp, w_down, w_up)
-
-
-def below_kernel(first_ref, second_ref, w_ref, gain_ref, term_ref, o_ref):
+    )(me, *pieces, *grad_pieces, gain_mlp, packed, packed)
+
+
+def below_kernel(me, first_ref, second_ref, w_ref, gain_ref, term_ref, o_ref):
     grad = contract_last(jnp.concatenate([first_ref[...], second_ref[...]], axis=1), w_ref[...])
     o_ref[...] = (grad * gain_ref[...] + term_ref[...].astype(F32)).astype(BF16)
 
 
-def below(first, second, weight, gain, term, block=512):
+def below(me, flip, first, second, weight, gain, term):
     length, half = first.shape
+    block = length // 4
     dim = weight.shape[0]
-    part = lambda i: (i, 0)
-    whole = lambda i: (0, 0)
+    part = lambda i, me: (2 * i + ((me[0] & 1) ^ flip), 0)
+    whole = lambda i, me: (0, 0)
     return pl.pallas_call(
         below_kernel,
         name="below",
-        grid=(length // block,),
-        in_specs=[
-            pl.BlockSpec((block, half), part),
-            pl.BlockSpec((block, half), part),
-            pl.BlockSpec((dim, 2 * half), whole),
-            pl.BlockSpec((1, dim), whole),
-            pl.BlockSpec((block, dim), part),
-        ],
-        out_specs=pl.BlockSpec((block, dim), part),
-        out_shape=jax.ShapeDtypeStruct((length, dim), BF16),
+        grid_spec=pltpu.PrefetchScalarGridSpec(
+            num_scalar_prefetch=1,
+            grid=(2,),
+            in_specs=[
+                pl.BlockSpec((block, half), part),
+                pl.BlockSpec((block, half), part),
+                pl.BlockSpec((dim, 2 * half), whole),
+                pl.BlockSpec((1, dim), whole),
+                pl.BlockSpec((block, dim), part),
+            ],
+            out_specs=pl.BlockSpec((block, dim), lambda i, me: (i, 0)),
+        ),
+        out_shape=jax.ShapeDtypeStruct((2 * block, dim), BF16),
         cost_estimate=pl.CostEstimate(
-            flops=4 * length * dim * half, bytes_accessed=4 * length * dim + 4 * length * half, transcendentals=0
-        ),
-    )(first, second, weight, gain, term)
+            flops=2 * length * dim * half, bytes_accessed=2 * length * dim + 2 * length * half, transcendentals=0
+        ),
+    )(me, first, second, weight, gain, term)
 
 
 def swap(values, axis, bit):
@@ -529,13 +565,7 @@
     )
     packed = [jnp.concatenate([local_up[:, k], local_down[k]], axis=1) for k in range(2)]
     first = lax.all_gather(packed[0], "fsdp")
-    first = first.transpose(1, 0, 2, 3)
     second = gather_far_first(packed[1], "fsdp", 1).reshape(ways, fold, 2 * rows, half)
-
-    def unpack(both):
-        up = both[:, :, :rows].reshape(dim, half)
-        down = both[:, :, rows:].reshape(2, 2, fold, rows, half).transpose(2, 1, 3, 0, 4)
-        return up, down.reshape(half, dim)
 
     local_rows = layer_input[0]
     row_pieces = gather_sequence(local_rows)
@@ -552,9 +582,8 @@
     tables = rotary_tables(length)
     gains, tables = lax.optimization_barrier((gains, tables))
 
-    up_first, down_first = unpack(first)
     normed_mlp, activated, grad_hidden, upstream, partial, mlp_term = mlp(
-        me, row_pieces, grad_pieces, gains[1:2], down_first, up_first
+        me, row_pieces, grad_pieces, gains[1:2], first
     )
 
     def feed_gradients(activated, grad_hidden):
@@ -566,10 +595,9 @@
         )
 
     grads_first = feed_gradients(activated, grad_hidden)
-    up_second, down_second = unpack(second)
     grads_first, partial = lax.optimization_barrier((grads_first, partial))
     activated, grad_hidden, partial, mlp_term = mlp_second(
-        normed_mlp, upstream, partial, mlp_term, gains[1:2], down_second, up_second
+        normed_mlp, upstream, partial, mlp_term, gains[1:2], second
     )
     grads_second = feed_gradients(activated, grad_hidden)
     sendable = jnp.concatenate(
@@ -592,13 +620,22 @@
     grad_pairs = []
     for pair in range(count):
         grad_pair = attend_back(qkv, context, grad_context, lse, tables, pair)
+        grad_pairs.append(grad_pair)
+        if pair + 1 == count:
+            sent = below(me, 1, *grad_pairs, full_qkv, gains[0:1], mlp_term)
+            grad_pair, sent = lax.optimization_barrier((grad_pair, sent))
         grad_weight = contract_first(normed_attn, grad_pair).astype(BF16)
         if pair + 1 < count:
             grad_weight, grad_context = lax.optimization_barrier((grad_weight, grad_context))
         near = reduce_near_first(grad_weight.reshape(ways, fold, rows, 3 * PAIR), "fsdp", 1)
         near_pairs.append(near)
-        grad_pairs.append(grad_pair)
-    upper = below(grad_pairs[0], grad_pairs[1], full_qkv, gains[0:1], mlp_term)
+    arrived = swap(sent, "seq", 1)
+    kept = below(me, 0, *grad_pairs, full_qkv, gains[0:1], mlp_term)
+    held = (kept.astype(F32) + arrived.astype(F32)).astype(BF16).reshape(2, tokens, dim)
+    mine = lax.axis_index("seq") >> 1
+    outward = pick(held, 1 - mine, 0)
+    inward = jnp.concatenate([swap(outward[: tokens // 2], "seq", 2), swap(outward[tokens // 2 :], "seq", 2)])
+    upper = pick(held, mine, 0).astype(F32) + inward.astype(F32)
     sum_down = owned_sum[:down_rows].astype(F32)
     back_up = exchange(owned_sum[down_rows:].reshape(ways, rows, hid), "seq")
     sum_up = (
@@ -610,7 +647,6 @@
         back_qkv.reshape(ways, rows, count, 3, PAIR).transpose(1, 3, 0, 2, 4).reshape(rows, 3 * inner).astype(F32)
     )
 
-    upper = sum_sequence(upper)
     local = local_rows.astype(F32)
     centred = local - jnp.mean(local, axis=-1, keepdims=True)
     inverse = lax.rsqrt(jnp.mean(centred * centred, axis=-1, keepdims=True) + EPS_NORM)

time: 449 us -> 445 us (level)
  waiting for transfers between devices: 168 us -> 161 us
  other arithmetic: 28.9 us -> 33.9 us
  local copies, waits for them, and re-layouts: 33.3 us -> 28.8 us
    ppermute x39 -> x40, waiting for transfers between devices: 167 us -> 157 us  [swap(): return lax.ppermute(values, axis, [(i, i ^ bit) for i in range(ways)])]
    convert_element_type x0 -> x2, other arithmetic: none -> 6.01 us  [the longest x1 3.46 us: one_step(): input_grad = (out_grad[0].astype(F32) + term).astype(BF16)[None]]
    pallas_call x1 -> x2, Pallas kernels: 8.48 us -> 10.7 us  [below(): pl.pallas_call(below_kernel, name='below', grid_spec=pltpu.PrefetchScalar...]
    ppermute x39 -> x40, starting transfers between devices: 34.5 us -> 34.7 us  [swap(): return lax.ppermute(values, axis, [(i, i ^ bit) for i in range(ways)])]
  transfers between devices with their start and end apart: 42 -> 43, of which waited for: 20 -> 19; matrix products, arithmetic and copies ran while one was open for 12% -> 12% of each run, Pallas kernels for 7% -> 8%
where the time goes in v2:
time: 445 us; the launch traced here: 439 us
  waiting for transfers between devices  161 us (36%)
  Pallas kernels  131 us (29%)
  starting transfers between devices  34.8 us (8%)
  other arithmetic  33.9 us (8%)
  matrix products  33.7 us (8%)
  local copies, waits for them, and re-layouts  28.8 us (6%)
  between operations  14.9 us (3%)
    ppermute x40, waiting for transfers between devices, swap(): return lax.ppermute(values, axis, [(i, i ^ bit) for i in range(ways)])  157 us
    pallas_call x2, Pallas kernels, attend_back(): pl.pallas_call(functools.partial(backward_kernel, block), name='attend_ba...  46.7 us
    ppermute x40, starting transfers between devices, swap(): return lax.ppermute(values, axis, [(i, i ^ bit) for i in range(ways)])  34.7 us
    pallas_call x1, Pallas kernels, attend(): pl.pallas_call(functools.partial(forward_kernel, block), name='attend', g...  26.6 us
    dot_general x7, matrix products, contract_first(): lax.dot_general(left, right, (((0,), (0,)), ((), ())), preferred_element_...  25.8 us
    pallas_call x1, Pallas kernels, mlp(): pl.pallas_call(functools.partial(mlp_kernel, count), name='mlp', grid_spe...  19.4 us
    pallas_call x1, Pallas kernels, mlp_second(): pl.pallas_call(second_kernel, name='mlp_second', grid=(length // block,),...  15.8 us
    pallas_call x1, Pallas kernels, project(): pl.pallas_call(functools.partial(project_kernel, count), name='project',...  12.1 us
  transfers between devices with their start and end apart: 43, of which 19 were waited for; matrix products, arithmetic and copies ran while one was open for 12% of the time, Pallas kernels for 8%

profile of v2, /device:TPU:0, one launch (start us, length us, event | category | flops | bytes accessed | tf_op | source)
XLA Modules:
  0.0 438.9 jit_solution(12542829477308519896)
XLA Ops:
  21.9 5.5 %multiply_sine_fusion = (f32[2048,128]{1,0:T(8,128)}, f32[2048,128]{1,0:T(8,128)}) fusion(f32[128]{0:T(128)S(1)} %compare_select_fusion.2, f32[2048]{0:T(1024)S(1)} %iota_convert_fusion), kind=kLoop, calls=%fused_computation.28 | loop fusion | flops 262144 | bytes 2105856 | tf_op jit(solution)/shard_map/sin | solution.py:523
  27.4 15.6 %collective-permute-done.13 = bf16[2,32,512]{2,1,0:T(8,128)(2,1)S(1)} collective-permute-done((bf16[2,32,512]{2,1,0:T(8,128)(2,1)S(1)}, bf16[2,32,512]{2,1,0:T(8,128)(2,1)S(1)}, u32[]{:S(2)}, u32[]{:S(2)}) %collective-permute-start.13) | collective-permute-done | bytes 65568 | tf_op jit(solution)/shard_map/ppermute | solution.py:451
  50.1 24.4 %collective-permute-done.17 = bf16[4,64,512]{2,1,0:T(8,128)(2,1)S(1)} collective-permute-done((bf16[4,64,512]{2,1,0:T(8,128)(2,1)S(1)}, bf16[4,64,512]{2,1,0:T(8,128)(2,1)S(1)}, u32[]{:S(2)}, u32[]{:S(2)}) %collective-permute-start.17) | collective-permute-done | bytes 262176 | tf_op jit(solution)/shard_map/ppermute | solution.py:451
  77.3 10.9 %collective-permute-done.18 = bf16[4,2,64,512]{3,2,0,1:T(8,128)(2,1)S(1)} collective-permute-done((bf16[4,2,64,512]{3,2,0,1:T(8,128)(2,1)S(1)}, bf16[4,2,64,512]{3,2,0,1:T(8,128)(2,1)S(1)}, u32[]{:S(2)}, u32[]{:S(2)}) %collective-permute-start.18) | collective-permute-done | bytes 524320 | tf_op jit(solution)/shard_map/ppermute | solution.py:451
  95.2 26.9 %collective-permute-done.10 = bf16[2,2,2,2,2,32]{5,1,0,2,3,4:T(2,128)(2,1)S(1)} collective-permute-done((bf16[2,2,2,2,2,32]{5,1,0,2,3,4:T(2,128)(2,1)S(1)}, bf16[2,2,2,2,2,32]{5,1,0,2,3,4:T(2,128)(2,1)S(1)}, u32[]{:S(2)}, u32[]{:S(2)}) %collective-permute-start.10) | collective-permute-done | bytes 2080 | tf_op jit(solution)/shard_map/ppermute | solution.py:451
  129.9 4.5 %all-gather.5.cloned.1.call-done = bf16[32,64,512]{2,1,0:T(8,128)(2,1)} async-done(((bf16[4,64,512]{2,1,0:T(8,128)(2,1)}), bf16[32,64,512]{2,1,0:T(8,128)(2,1)}) %all-gather.5.cloned.1.call-update) | async-done | bytes 2097168 | tf_op jit(solution)/shard_map/all_gather | solution.py:567
  134.4 19.4 %mlp.1 = (bf16[2048,1024]{1,0:T(8,128)(2,1)}, bf16[2048,512]{1,0:T(8,128)(2,1)}, bf16[2048,512]{1,0:T(8,128)(2,1)}, bf16[2048,1024]{1,0:T(8,128)(2,1)}, bf16[204...) custom-call(s32[1]{0:T(128)} %bitcast.1.me, bf16[512,1024]{1,0:T(8,128)(2,1)} %bitcast.240, ...), custom_call_target="tpu_custom_call" | custom-call | flops 8589934592 | bytes 35651584 | tf_op jit(solution)/shard_map/mlp/pallas_call | solution.py:389
  153.9 5.4 %convolution_convert_fusion.3 = bf16[1024,512]{1,0:T(8,128)(2,1)S(1)} fusion(bf16[2048,1024]{1,0:T(8,128)(2,1)} %get-tuple-element.58.n_ref, bf16[2048,512]{1,0:T(8,128)(2,1)} %get-tuple-element.59), kind=kOutput, calls=%fused_computation.32 | convolution fusion | flops 2148007936 | bytes 7340032 | tf_op jit(solution)/shard_map/dot_general | solution.py:29
  163.2 15.8 %mlp_second.1 = (bf16[2048,512]{1,0:T(8,128)(2,1)}, bf16[2048,512]{1,0:T(8,128)(2,1)}, bf16[2048,1024]{1,0:T(8,128)(2,1)}, bf16[2048,1024]{1,0:T(8,128)(2,1)}) custom-call(bf16[2048,1024]{1,0:T(8,128)(2,1)} %get-tuple-element.58.n_ref, bf16[2048,1024]{1,0:T(8,128)(2,1)} %get-tuple-element.56.g_ref, bf16[2048,1024]{1,0:T(8,128)(2,1)} %get-tuple-element.62.part_in, ...), custom_call_target="tpu_custom_call" | custom-call | flops 8589934592 | bytes 35651584 | tf_op jit(solution)/shard_map/mlp_second/pallas_call | solution.py:344
  178.9 5.4 %convolution_convert_fusion.1 = bf16[1024,512]{1,0:T(8,128)(2,1)S(1)} fusion(bf16[2048,1024]{1,0:T(8,128)(2,1)} %get-tuple-element.58.n_ref, bf16[2048,512]{1,0:T(8,128)(2,1)} %get-tuple-element.66), kind=kOutput, calls=%fused_computation.30 | convolution fusion | flops 2148007936 | bytes 7340032 | tf_op jit(solution)/shard_map/dot_general | solution.py:29
  190.6 12.1 %project.1 = (bf16[2048,1024]{1,0:T(8,128)(2,1)}, bf16[2048,768]{1,0:T(8,128)(2,1)}) custom-call(s32[1]{0:T(128)} %bitcast.1.me, bf16[512,1024]{1,0:T(8,128)(2,1)} %bitcast.241, bf16[512,1024]{1,0:T(8,128)(2,1)} %collective-permute-done.x1, bf16[512,1024]{1,0:T(8,128)(2,1)} %collective-permute-done.1.x2, bf16[512,1024]{1,0:T(8,128)(2,1)} %collective-permute-done.2.x3, ...), custom_call_target="tpu_custom_call" | custom-call | flops 3221225472 | bytes 15728640 | tf_op jit(solution)/shard_map/project/pallas_call | solution.py:101
  202.7 26.6 %attend.1 = (bf16[2048,256]{1,0:T(8,128)(2,1)}, f32[2048,256]{1,0:T(8,128)}) custom-call(bf16[2048,768]{1,0:T(8,128)(2,1)} %get-tuple-element.70.q_ref.k_ref.v_ref, bf16[2048,768]{1,0:T(8,128)(2,1)} %get-tuple-element.70.q_ref.k_ref.v_ref, bf16[2048,768]{1,0:T(8,128)(2,1)} %get-tuple-element.70.q_ref.k_ref.v_ref), custom_call_target="tpu_custom_call" | custom-call | flops 8589934592 | bytes 6291456 | tf_op jit(solution)/shard_map/attend/pallas_call | solution.py:182
  229.3 4.6 %convolution_convert_fusion.do_ref = bf16[2048,256]{1,0:T(8,128)(2,1)} fusion(bf16[2048,1024]{1,0:T(8,128)(2,1)} %get-tuple-element.56.g_ref, bf16[256,1024]{1,0:T(8,128)(2,1)S(1)} %bitcast.253), kind=kOutput, calls=%fused_computation.10 | convolution fusion | flops 1074266112 | bytes 5767168 | tf_op jit(solution)/shard_map/dot_general | solution.py:25
  239.5 23.4 %attend_back.2.first_ref = bf16[2048,384]{1,0:T(8,128)(2,1)} custom-call(bf16[2048,768]{1,0:T(8,128)(2,1)} %get-tuple-element.70.q_ref.k_ref.v_ref, bf16[2048,768]{1,0:T(8,128)(2,1)} %get-tuple-element.70.q_ref.k_ref.v_ref, bf16[2048,768]{1,0:T(8,128)(2,1)} %get-tuple-element.70.q_ref.k_ref.v_ref, bf16[2048,256]{1,0:T(8,128)(2,1)} %get-tuple-element.71.o_ref, ...), custom_call_target="tpu_custom_call" | custom-call | flops 10737418240 | bytes 5242880 | tf_op jit(solution)/shard_map/attend_back/pallas_call | solution.py:275
  262.9 5.0 %convolution_convert_fusion.6 = bf16[1024,384]{1,0:T(8,128)(2,1)S(1)} fusion(bf16[2048,1024]{1,0:T(8,128)(2,1)} %get-tuple-element.76, bf16[2048,384]{1,0:T(8,128)(2,1)} %attend_back.2.first_ref), kind=kOutput, calls=%fused_computation.35 | convolution fusion | flops 1611005952 | bytes 6553600 | tf_op jit(solution)/shard_map/dot_general | solution.py:29
  267.9 23.3 %attend_back.3.second_ref = bf16[2048,384]{1,0:T(8,128)(2,1)} custom-call(bf16[2048,768]{1,0:T(8,128)(2,1)} %get-tuple-element.70.q_ref.k_ref.v_ref, bf16[2048,768]{1,0:T(8,128)(2,1)} %get-tuple-element.70.q_ref.k_ref.v_ref, bf16[2048,768]{1,0:T(8,128)(2,1)} %get-tuple-element.70.q_ref.k_ref.v_ref, bf16[2048,256]{1,0:T(8,128)(2,1)} %get-tuple-element.71.o_ref, ...), custom_call_target="tpu_custom_call" | custom-call | flops 10737418240 | bytes 5242880 | tf_op jit(solution)/shard_map/attend_back/pallas_call | solution.py:275
  291.3 5.3 %below.3 = bf16[1024,1024]{1,0:T(8,128)(2,1)} custom-call(s32[1]{0:T(128)} %bitcast.1.me, bf16[2048,384]{1,0:T(8,128)(2,1)} %attend_back.2.first_ref, bf16[2048,384]{1,0:T(8,128)(2,1)} %attend_back.3.second_ref, bf16[1024,768]{1,0:T(8,128)(2,1)} %bitcast.245, f32[1,1024]{1,0:T(1,128)} %get-tuple-element.147.ga_ref.gain_ref, ...), custom_call_target="tpu_custom_call" | custom-call | flops 1610612736 | bytes 5767168 | tf_op jit(solution)/shard_map/below/pallas_call | solution.py:427
  307.2 5.4 %below.2 = bf16[1024,1024]{1,0:T(8,128)(2,1)} custom-call(s32[1]{0:T(128)} %bitcast.1.me, bf16[2048,384]{1,0:T(8,128)(2,1)} %attend_back.2.first_ref, bf16[2048,384]{1,0:T(8,128)(2,1)} %attend_back.3.second_ref, bf16[1024,768]{1,0:T(8,128)(2,1)} %bitcast.246, f32[1,1024]{1,0:T(1,128)} %get-tuple-element.147.ga_ref.gain_ref, ...), custom_call_target="tpu_custom_call" | custom-call | flops 1610612736 | bytes 5767168 | tf_op jit(solution)/shard_map/below/pallas_call | solution.py:427
  314.5 10.7 %collective-permute-done.34 = bf16[2,2,32,1024]{3,2,0,1:T(8,128)(2,1)} collective-permute-done((bf16[2,2,32,1024]{3,2,0,1:T(8,128)(2,1)}, bf16[2,2,32,1024]{3,2,0,1:T(8,128)(2,1)}, u32[]{:S(2)}, u32[]{:S(2)}) %collective-permute-start.34) | collective-permute-done | bytes 262176 | tf_op jit(solution)/shard_map/ppermute | solution.py:451
  328.7 9.0 %collective-permute-done.28 = bf16[4,2,2,32,384]{4,3,0,1,2:T(8,128)(2,1)S(1)} collective-permute-done((bf16[4,2,2,32,384]{4,3,0,1,2:T(8,128)(2,1)S(1)}, bf16[4,2,2,32,384]{4,3,0,1,2:T(8,128)(2,1)S(1)}, u32[]{:S(2)}, u32[]{:S(2)}) %collective-permute-start.28) | collective-permute-done | bytes 393248 | tf_op jit(solution)/shard_map/ppermute | solution.py:451
  347.6 5.2 %collective-permute-done.27 = bf16[4,32,384]{2,1,0:T(8,128)(2,1)S(1)} collective-permute-done((bf16[4,32,384]{2,1,0:T(8,128)(2,1)S(1)}, bf16[4,32,384]{2,1,0:T(8,128)(2,1)S(1)}, u32[]{:S(2)}, u32[]{:S(2)}) %collective-permute-start.27) | collective-permute-done | bytes 98336 | tf_op jit(solution)/shard_map/ppermute | solution.py:451
  352.9 6.5 %collective-permute-done.30 = bf16[4,32,384]{2,1,0:T(8,128)(2,1)S(1)} collective-permute-done((bf16[4,32,384]{2,1,0:T(8,128)(2,1)S(1)}, bf16[4,32,384]{2,1,0:T(8,128)(2,1)S(1)}, u32[]{:S(2)}, u32[]{:S(2)}) %collective-permute-start.30) | collective-permute-done | bytes 98336 | tf_op jit(solution)/shard_map/ppermute | solution.py:451
  381.4 22.8 %collective-permute-done.24 = bf16[256,1024]{1,0:T(8,128)(2,1)} collective-permute-done((bf16[256,1024]{1,0:T(8,128)(2,1)}, bf16[256,1024]{1,0:T(8,128)(2,1)}, u32[]{:S(2)}, u32[]{:S(2)}) %collective-permute-start.24) | collective-permute-done | bytes 524320 | tf_op jit(solution)/shard_map/ppermute | solution.py:451
  404.2 10.4 %collective-permute-done.23 = bf16[256,1024]{1,0:T(8,128)(2,1)} collective-permute-done((bf16[256,1024]{1,0:T(8,128)(2,1)}, bf16[256,1024]{1,0:T(8,128)(2,1)}, u32[]{:S(2)}, u32[]{:S(2)}) %collective-permute-start.23) | collective-permute-done | bytes 524320 | tf_op jit(solution)/shard_map/ppermute | solution.py:451
  (256 shorter events, 119.8 us)
Async XLA Ops:
  7.2 118.2 %all-gather.7.cloned.1.call-start = ((), (), s32[]{:S(2)}) async-start(), calls=%async_computation.3 | async-start | bytes 2359296 | tf_op jit(solution)/shard_map/all_gather | solution.py:579
  16.5 118.0 %all-gather.5.cloned.1.call-start = ((), (), s32[]{:S(2)}) async-start(), calls=%async_computation.2 | async-start | bytes 2359296 | tf_op jit(solution)/shard_map/all_gather | solution.py:567
  16.5 113.3 %collective-permute-start = (bf16[512,1024]{1,0:T(8,128)(2,1)S(1)}, bf16[512,1024]{1,0:T(8,128)(2,1)}, u32[]{:S(2)}, u32[]{:S(2)}) collective-permute-start(bf16[512,1024]{1,0:T(8,128)(2,1)S(1)} %bitcast.242), channel_id=1, source_target_pairs={{0,8},{8,0},{16,24},{24,16},{1,9},{9,1},{17,25},{25,17},{2,10},{10... | collective-permute-start | bytes 3145736 | tf_op jit(solution)/shard_map/ppermute | solution.py:451
  16.6 105.6 %collective-permute-start.1 = (bf16[512,1024]{1,0:T(8,128)(2,1)S(1)}, bf16[512,1024]{1,0:T(8,128)(2,1)}, u32[]{:S(2)}, u32[]{:S(2)}) collective-permute-start(bf16[512,1024]{1,0:T(8,128)(2,1)S(1)} %bitcast.243), channel_id=1, source_target_pairs={{0,16},{8,24},{16,0},{24,8},{1,17},{9,25},{17,1},{25,9},{2,18},{10... | collective-permute-start | bytes 3145736 | tf_op jit(solution)/shard_map/ppermute | solution.py:451
  19.0 24.0 %collective-permute-start.13 = (bf16[2,32,512]{2,1,0:T(8,128)(2,1)S(1)}, bf16[2,32,512]{2,1,0:T(8,128)(2,1)S(1)}, u32[]{:S(2)}, u32[]{:S(2)}) collective-permute-start(bf16[2,32,512]{2,1,0:T(8,128)(2,1)S(1)} %get-tuple-element.132), channel_id=1, source_target_pairs={{0,24},{8,16},{16,8},{24,0},{1,25},{9,17},{17,9},{25,1},{2,26},{10... | collective-permute-start | bytes 196616 | tf_op jit(solution)/shard_map/ppermute | solution.py:451
  19.5 25.5 %collective-permute-start.12 = (bf16[2,32,512]{2,1,0:T(8,128)(2,1)S(1)}, bf16[2,32,512]{2,1,0:T(8,128)(2,1)S(1)}, u32[]{:S(2)}, u32[]{:S(2)}) collective-permute-start(bf16[2,32,512]{2,1,0:T(8,128)(2,1)S(1)} %get-tuple-element.133), channel_id=1, source_target_pairs={{0,16},{8,24},{16,0},{24,8},{1,17},{9,25},{17,1},{25,9},{2,18},{10... | collective-permute-start | bytes 196616 | tf_op jit(solution)/shard_map/ppermute | solution.py:451
  20.9 25.5 %collective-permute-start.11 = (bf16[2,32,512]{2,1,0:T(8,128)(2,1)S(1)}, bf16[2,32,512]{2,1,0:T(8,128)(2,1)S(1)}, u32[]{:S(2)}, u32[]{:S(2)}) collective-permute-start(bf16[2,32,512]{2,1,0:T(8,128)(2,1)S(1)} %get-tuple-element.134), channel_id=1, source_target_pairs={{0,8},{8,0},{16,24},{24,16},{1,9},{9,1},{17,25},{25,17},{2,10},{10... | collective-permute-start | bytes 196616 | tf_op jit(solution)/shard_map/ppermute | solution.py:451
  45.0 77.9 %collective-permute-start.4 = (bf16[512,1024]{1,0:T(8,128)(2,1)}, bf16[512,1024]{1,0:T(8,128)(2,1)}, u32[]{:S(2)}, u32[]{:S(2)}) collective-permute-start(bf16[512,1024]{1,0:T(8,128)(2,1)} %bitcast.2.g0), channel_id=1, source_target_pairs={{0,16},{8,24},{16,0},{24,8},{1,17},{9,25},{17,1},{25,9},{2,18},{10... | collective-permute-start | bytes 3145736 | tf_op jit(solution)/shard_map/ppermute | solution.py:451
  46.6 28.0 %collective-permute-start.17 = (bf16[4,64,512]{2,1,0:T(8,128)(2,1)S(1)}, bf16[4,64,512]{2,1,0:T(8,128)(2,1)S(1)}, u32[]{:S(2)}, u32[]{:S(2)}) collective-permute-start(bf16[4,64,512]{2,1,0:T(8,128)(2,1)S(1)} %pad_maximum_fusion.7), channel_id=1, source_target_pairs={{0,4},{1,5},{2,6},{3,7},{4,0},{5,1},{6,2},{7,3},{8,12},{9,13},{10,... | collective-permute-start | bytes 786440 | tf_op jit(solution)/shard_map/ppermute | solution.py:451
  50.0 371.6 %reduce-scatter.2.cloned.1.call-start = ((), (), s32[]{:S(2)}) async-start(), calls=%async_computation.1 | async-start | bytes 4718592 | tf_op jit(solution)/shard_map/reduce_scatter | solution.py:607
  50.0 24.7 %collective-permute-start.7 = (bf16[2,2,32]{2,0,1:T(2,128)(2,1)S(1)}, bf16[2,2,32]{2,0,1:T(2,128)(2,1)S(1)}, u32[]{:S(2)}, u32[]{:S(2)}) collective-permute-start(bf16[2,2,32]{2,0,1:T(2,128)(2,1)S(1)} %pad_maximum_fusion.14), channel_id=1, source_target_pairs={{0,8},{8,0},{16,24},{24,16},{1,9},{9,1},{17,25},{25,17},{2,10},{10... | collective-permute-start | bytes 776 | tf_op jit(solution)/shard_map/ppermute | solution.py:451
  74.7 13.5 %collective-permute-start.18 = (bf16[4,2,64,512]{3,2,0,1:T(8,128)(2,1)S(1)}, bf16[4,2,64,512]{3,2,0,1:T(8,128)(2,1)S(1)}, u32[]{:S(2)}, u32[]{:S(2)}) collective-permute-start(bf16[4,2,64,512]{3,2,0,1:T(8,128)(2,1)S(1)} %pad_maximum_fusion.3), channel_id=1, source_target_pairs={{0,2},{1,3},{2,0},{3,1},{4,6},{5,7},{6,4},{7,5},{8,10},{9,11},{10,... | collective-permute-start | bytes 1572872 | tf_op jit(solution)/shard_map/ppermute | solution.py:451
  74.8 16.0 %collective-permute-start.8 = (bf16[2,2,2,32]{3,1,0,2:T(2,128)(2,1)S(1)}, bf16[2,2,2,32]{3,1,0,2:T(2,128)(2,1)S(1)}, u32[]{:S(2)}, u32[]{:S(2)}) collective-permute-start(bf16[2,2,2,32]{3,1,0,2:T(2,128)(2,1)S(1)} %pad_maximum_fusion.13), channel_id=1, source_target_pairs={{0,4},{1,5},{2,6},{3,7},{4,0},{5,1},{6,2},{7,3},{8,12},{9,13},{10,... | collective-permute-start | bytes 1544 | tf_op jit(solution)/shard_map/ppermute | solution.py:451
  89.3 34.2 %collective-permute-start.19 = (bf16[4,2,2,64,512]{4,3,0,1,2:T(8,128)(2,1)}, bf16[4,2,2,64,512]{4,3,0,1,2:T(8,128)(2,1)S(1)}, u32[]{:S(2)}, u32[]{:S(2)}) collective-permute-start(bf16[4,2,2,64,512]{4,3,0,1,2:T(8,128)(2,1)} %pad_maximum_fusion.1), channel_id=1, source_target_pairs={{0,1},{1,0},{2,3},{3,2},{4,5},{5,4},{6,7},{7,6},{8,9},{9,8},{10,11... | collective-permute-start | bytes 3145736 | tf_op jit(solution)/shard_map/ppermute | solution.py:451
  94.7 27.4 %collective-permute-start.10 = (bf16[2,2,2,2,2,32]{5,1,0,2,3,4:T(2,128)(2,1)S(1)}, bf16[2,2,2,2,2,32]{5,1,0,2,3,4:T(2,128)(2,1)S(1)}, u32[]{:S(2)}, u32[]{:S(2)}) collective-permute-start(bf16[2,2,2,2,2,32]{5,1,0,2,3,4:T(2,128)(2,1)S(1)} %pad_maximum_fusion.11), channel_id=1, source_target_pairs={{0,1},{1,0},{2,3},{3,2},{4,5},{5,4},{6,7},{7,6},{8,9},{9,8},{10,11... | collective-permute-start | bytes 6152 | tf_op jit(solution)/shard_map/ppermute | solution.py:451
  296.6 71.0 %collective-permute-start.22 = (bf16[1024,1024]{1,0:T(8,128)(2,1)}, bf16[1024,1024]{1,0:T(8,128)(2,1)}, u32[]{:S(2)}, u32[]{:S(2)}) collective-permute-start(bf16[1024,1024]{1,0:T(8,128)(2,1)} %below.3), channel_id=1, source_target_pairs={{0,8},{8,0},{16,24},{24,16},{1,9},{9,1},{17,25},{25,17},{2,10},{10... | collective-permute-start | bytes 6291464 | tf_op jit(solution)/shard_map/ppermute | solution.py:451
  299.8 64.7 %collective-permute-start.20 = (bf16[2,512,1024]{2,1,0:T(8,128)(2,1)}, bf16[2,512,1024]{2,1,0:T(8,128)(2,1)S(1)}, u32[]{:S(2)}, u32[]{:S(2)}) collective-permute-start(bf16[2,512,1024]{2,1,0:T(8,128)(2,1)} %dynamic-slice_bitcast_fusion), channel_id=1, source_target_pairs={{0,8},{8,0},{16,24},{24,16},{1,9},{9,1},{17,25},{25,17},{2,10},{10... | collective-permute-start | bytes 6291464 | tf_op jit(solution)/shard_map/ppermute | solution.py:451
  301.1 26.5 %collective-permute-start.25 = (bf16[4,2,2,32,384]{4,3,2,1,0:T(8,128)(2,1)}, bf16[4,2,2,32,384]{4,3,2,1,0:T(8,128)(2,1)S(1)}, u32[]{:S(2)}, u32[]{:S(2)}) collective-permute-start(bf16[4,2,2,32,384]{4,3,2,1,0:T(8,128)(2,1)} %dynamic-slice_bitcast_fusion.4), channel_id=1, source_target_pairs={{0,1},{1,0},{2,3},{3,2},{4,5},{5,4},{6,7},{7,6},{8,9},{9,8},{10,11... | collective-permute-start | bytes 1179656 | tf_op jit(solution)/shard_map/ppermute | solution.py:451
  302.4 22.8 %collective-permute-start.34 = (bf16[2,2,32,1024]{3,2,0,1:T(8,128)(2,1)}, bf16[2,2,32,1024]{3,2,0,1:T(8,128)(2,1)}, u32[]{:S(2)}, u32[]{:S(2)}) collective-permute-start(bf16[2,2,32,1024]{3,2,0,1:T(8,128)(2,1)} %bitcast.235), channel_id=1, source_target_pairs={{0,1},{1,0},{2,3},{3,2},{4,5},{5,4},{6,7},{7,6},{8,9},{9,8},{10,11... | collective-permute-start | bytes 786440 | tf_op jit(solution)/shard_map/ppermute | solution.py:451
  313.9 23.7 %collective-permute-start.28 = (bf16[4,2,2,32,384]{4,3,0,1,2:T(8,128)(2,1)S(1)}, bf16[4,2,2,32,384]{4,3,0,1,2:T(8,128)(2,1)S(1)}, u32[]{:S(2)}, u32[]{:S(2)}) collective-permute-start(bf16[4,2,2,32,384]{4,3,0,1,2:T(8,128)(2,1)S(1)} %bitcast.282), channel_id=1, source_target_pairs={{0,1},{1,0},{2,3},{3,2},{4,5},{5,4},{6,7},{7,6},{8,9},{9,8},{10,11... | collective-permute-start | bytes 1179656 | tf_op jit(solution)/shard_map/ppermute | solution.py:451
  339.4 21.4 %collective-permute-start.36 = (bf16[32,1024]{1,0:T(8,128)(2,1)S(1)}, bf16[32,1024]{1,0:T(8,128)(2,1)S(1)}, u32[]{:S(2)}, u32[]{:S(2)}) collective-permute-start(bf16[32,1024]{1,0:T(8,128)(2,1)S(1)} %dynamic-slice_bitcast_fusion.13), channel_id=1, source_target_pairs={{0,4},{1,5},{2,6},{3,7},{4,0},{5,1},{6,2},{7,3},{8,12},{9,13},{10,... | collective-permute-start | bytes 196616 | tf_op jit(solution)/shard_map/ppermute | solution.py:451
  366.7 48.0 %collective-permute-start.21 = (bf16[512,1024]{1,0:T(8,128)(2,1)}, bf16[512,1024]{1,0:T(8,128)(2,1)}, u32[]{:S(2)}, u32[]{:S(2)}) collective-permute-start(bf16[512,1024]{1,0:T(8,128)(2,1)} %dynamic-slice_bitcast_fusion.1), channel_id=1, source_target_pairs={{0,16},{8,24},{16,0},{24,8},{1,17},{9,25},{17,1},{25,9},{2,18},{10... | collective-permute-start | bytes 3145736 | tf_op jit(solution)/shard_map/ppermute | solution.py:451
  371.9 32.3 %collective-permute-start.24 = (bf16[256,1024]{1,0:T(8,128)(2,1)}, bf16[256,1024]{1,0:T(8,128)(2,1)}, u32[]{:S(2)}, u32[]{:S(2)}) collective-permute-start(bf16[256,1024]{1,0:T(8,128)(2,1)} %get-tuple-element.109), channel_id=1, source_target_pairs={{0,16},{8,24},{16,0},{24,8},{1,17},{9,25},{17,1},{25,9},{2,18},{10... | collective-permute-start | bytes 1572872 | tf_op jit(solution)/shard_map/ppermute | solution.py:451
  372.9 41.7 %collective-permute-start.23 = (bf16[256,1024]{1,0:T(8,128)(2,1)}, bf16[256,1024]{1,0:T(8,128)(2,1)}, u32[]{:S(2)}, u32[]{:S(2)}) collective-permute-start(bf16[256,1024]{1,0:T(8,128)(2,1)} %get-tuple-element.108), channel_id=1, source_target_pairs={{0,16},{8,24},{16,0},{24,8},{1,17},{9,25},{17,1},{25,9},{2,18},{10... | collective-permute-start | bytes 1572872 | tf_op jit(solution)/shard_map/ppermute | solution.py:451
  (51 other events, 455.0 us)
Sparse Core Ops, SparseCore 0:
  16.6 59.3 all-gather.6
  78.7 55.6 all-gather.4
  268.1 103.0 reduce-scatter.1
